TPU v7x, 256 devices: a whole 4x4x8 slice. The times are simulated.
256 devices in a mesh: ctx: 32 (over z, y), tp: 4 (over x), fsdp: 2 (over core).
Axes of the slice: x: 4, y: 4, z: 8, core: 2. Of those that a mesh axis runs over, the one named last changes fastest.
Arguments:
- tokens: bfloat16 [2, 32768, 2048], P('fsdp', 'ctx'), may hold values from -6 to 6
- query_weight: bfloat16 [2048, 2048], P('fsdp', 'tp'), may hold values from -0.125 to 0.125
- key_weight: bfloat16 [2048, 2048], P('fsdp', 'tp'), may hold values from -0.125 to 0.125
- value_weight: bfloat16 [2048, 2048], P('fsdp', 'tp'), may hold values from -0.125 to 0.125
- gate_weight: bfloat16 [2048, 2048], P('fsdp', 'tp'), may hold values from -0.125 to 0.125
- out_weight: bfloat16 [2048, 2048], P('tp', 'fsdp'), may hold values from -0.125 to 0.125
- log_decay: float32 [2, 32768, 8], P('fsdp', 'ctx', 'tp'), may hold values from -1 to 0
Outputs:
- mixed: bfloat16 [2, 32768, 2048], P('fsdp', 'ctx', 'tp')
All inputs are finite; a program needn't handle non-finite values.
Results may differ from a plain program's by a relative error of at most 0.013.
Values may be sent and summed in bfloat16 or wider, within the bound.
A program may use at most 128 MiB of HBM per device.

v0:
```python
import jax
import jax.numpy as jnp
from jax import lax
from jax.sharding import PartitionSpec as P

DH = 256
BLOCK = 512


def entering(value, axis, join, neutral):
    count, mine = (lax.axis_size(axis), lax.axis_index(axis))
    pieces = jax.tree.map(lambda part: lax.all_gather(part, axis), value)
    running = jax.tree.map(
        lambda part, zero: jnp.full_like(part, 0) + jnp.asarray(zero, part.dtype), value, neutral
    )

    def hop(position, running):
        longer = join(running, jax.tree.map(lambda part: part[position], pieces))
        return jax.tree.map(lambda new, old: jnp.where(position < mine, new, old), longer, running)

    return lax.fori_loop(0, count - 1, hop, running)


def rotate(values, positions):
    half_dim = values.shape[-1] // 2
    index_row = jnp.arange(half_dim).astype(jnp.float32)
    frequency = jnp.power(jnp.float32(10000.0), -index_row / half_dim)
    angles = positions[:, None] * frequency[None, :]
    cosine = jnp.concatenate([jnp.cos(angles), jnp.cos(angles)], axis=-1)[:, None, :]
    sine_part = jnp.concatenate([jnp.sin(angles), jnp.sin(angles)], axis=-1)[:, None, :]
    turned = jnp.concatenate([-values[..., half_dim:], values[..., :half_dim]], axis=-1)
    return values * cosine + turned * sine_part


def group_norm(retained):
    center = retained - jnp.mean(retained, axis=-1, keepdims=True)
    spread = jnp.mean(center * center, axis=-1, keepdims=True)
    return center * lax.rsqrt(spread + 1e-05)


def combine(earlier, later):
    return (earlier[0] + later[0], jnp.exp(later[0])[:, None, None] * earlier[1] + later[1])


def on_device(tokens, query_weight, key_weight, value_weight, gate_weight, out_weight, log_decay):
    token_rows = tokens[0]
    row_count = token_rows.shape[0]
    col_count = query_weight.shape[1]
    head_count = col_count // DH
    block_count = row_count // BLOCK

    def add_rows(shard_rows):
        return jnp.dot(token_rows, shard_rows, preferred_element_type=jnp.float32)

    query_proj = add_rows(lax.all_gather(query_weight, "fsdp", axis=0, tiled=True))
    key_proj = add_rows(lax.all_gather(key_weight, "fsdp", axis=0, tiled=True))
    value_proj = add_rows(lax.all_gather(value_weight, "fsdp", axis=0, tiled=True))
    gate_proj = add_rows(lax.all_gather(gate_weight, "fsdp", axis=0, tiled=True))
    offset = lax.axis_index("ctx") * row_count
    positions = (offset + jnp.arange(row_count)).astype(jnp.float32)
    block_shape = (block_count, BLOCK, head_count, DH)
    queries = (
        rotate(query_proj.reshape(row_count, head_count, DH), positions)
        .astype(jnp.bfloat16)
        .reshape(block_shape)
    )
    keys_block = (
        rotate(key_proj.reshape(row_count, head_count, DH), positions)
        .astype(jnp.bfloat16)
        .reshape(block_shape)
    )
    values_block = value_proj.astype(jnp.bfloat16).reshape(block_shape)
    gate_values = gate_proj.astype(jnp.bfloat16)
    cumulative = jnp.cumsum(log_decay[0].reshape(block_count, BLOCK, head_count), axis=1)
    scores = jnp.einsum("cthd,cshd->chts", queries, keys_block, preferred_element_type=jnp.float32)
    leading = jnp.transpose(cumulative, (0, 2, 1))
    differ = leading[:, :, :, None] - leading[:, :, None, :]
    causal = jnp.arange(BLOCK)[:, None] >= jnp.arange(BLOCK)[None, :]
    weights = jnp.where(causal, jnp.exp(jnp.where(causal, differ, 0.0)), 0.0)
    mixed_weights = (scores * weights).astype(jnp.bfloat16)
    intra_part = jnp.einsum(
        "chts,cshd->cthd", mixed_weights, values_block, preferred_element_type=jnp.float32
    )
    ending = cumulative[:, -1, :]
    weighted = keys_block.astype(jnp.float32) * jnp.exp(ending[:, None, :] - cumulative)[..., None]
    updates = jnp.einsum(
        "cshd,cshe->chde",
        weighted,
        values_block.astype(jnp.float32),
        precision=lax.Precision.HIGHEST,
    )
    device_total = jnp.sum(ending, axis=0)
    device_state = updates[0]
    block_index = 1
    device_state = jnp.exp(ending[block_index])[:, None, None] * device_state + updates[block_index]
    incoming = entering(
        (device_total, device_state),
        "ctx",
        combine,
        (jnp.zeros_like(device_total), jnp.zeros_like(device_state)),
    )
    carried = incoming[1]
    prior_states = []
    for block_index in range(block_count):
        prior_states.append(carried)
        carried = jnp.exp(ending[block_index])[:, None, None] * carried + updates[block_index]
    prior_stack = jnp.stack(prior_states)
    inter_part = jnp.exp(cumulative)[..., None] * jnp.einsum(
        "cthd,chde->cthe", queries.astype(jnp.float32), prior_stack, precision=lax.Precision.HIGHEST
    )
    retained = (intra_part + inter_part).reshape(row_count, head_count, DH)
    normed = group_norm(retained).reshape(row_count, col_count)
    hidden = (jax.nn.silu(gate_values.astype(jnp.float32)) * normed).astype(jnp.bfloat16)
    partial_terms = jnp.dot(
        hidden,
        lax.all_gather(out_weight, "fsdp", axis=1, tiled=True),
        preferred_element_type=jnp.float32,
    )
    result = lax.psum_scatter(partial_terms, "tp", scatter_dimension=1, tiled=True).astype(
        jnp.bfloat16
    )
    return result[None]


def solution(mesh):
    in_specs = (
        P("fsdp", "ctx", None),
        P("fsdp", "tp"),
        P("fsdp", "tp"),
        P("fsdp", "tp"),
        P("fsdp", "tp"),
        P("tp", "fsdp"),
        P("fsdp", "ctx", "tp"),
    )
    out_specs = P("fsdp", "ctx", "tp")
    return jax.shard_map(
        on_device, mesh=mesh, in_specs=in_specs, out_specs=out_specs, check_vma=False
    )
```

profile of v0, /device:TPU:8, one launch (start us, length us, event | category | flops | bytes accessed | tf_op | source)
XLA Modules:
  0.0 369.9 jit_solution(10420444462744150177)
XLA Ops:
  8.9 1.2 reduce-window.6
  11.2 1.9 multiply_cosine_fusion
  13.3 14.7 %all-gather.14.cloned.1.call-done = bf16[2048,512]{1,0:T(8,128)(2,1)} async-done(((bf16[1024,512]{1,0:T(8,128)(2,1)}), bf16[2048,512]{1,0:T(8,128)(2,1)}) %all-gather.14.cloned.1.call-update) | async-done | bytes 2097168 | tf_op jit(solution)/shard_map/all_gather | solution.py:56
  28.0 3.9 %copy.64 = bf16[512,2048]{1,0:T(8,128)(2,1)} copy(bf16[512,2048]{0,1:T(8,128)(2,1)} %bitcast.81) | data formatting | bytes 4194304 | tf_op jit(solution)/shard_map/dot_general | solution.py:53
  31.9 15.1 %all-gather.12.cloned.1.call-done = bf16[2048,512]{1,0:T(8,128)(2,1)} async-done(((bf16[1024,512]{1,0:T(8,128)(2,1)}), bf16[2048,512]{1,0:T(8,128)(2,1)}) %all-gather.12.cloned.1.call-update) | async-done | bytes 2097168 | tf_op jit(solution)/shard_map/all_gather | solution.py:55
  47.0 4.0 %copy.63 = bf16[512,2048]{1,0:T(8,128)(2,1)} copy(bf16[512,2048]{0,1:T(8,128)(2,1)} %bitcast.82) | data formatting | bytes 4194304 | tf_op jit(solution)/shard_map/dot_general | solution.py:53
  51.0 5.4 %fusion.1 = f32[1024,2,256]{2,0,1:T(8,128)S(1)} fusion(bf16[2,256,2048]{2,1,0:T(8,128)(2,1)} %bitcast.86, bf16[1,1024,2048]{2,1,0:T(8,128)(2,1)} %param.9), kind=kOutput, calls=%fused_computation.3 | convolution fusion | flops 2147483648 | bytes 8388608 | tf_op jit(solution)/shard_map/dot_general | solution.py:53
  56.4 2.4 fusion.3
  59.1 1.6 fusion.14
  61.2 4.9 %all-gather.10.cloned.1.call-done = bf16[2048,512]{1,0:T(8,128)(2,1)} async-done(((bf16[1024,512]{1,0:T(8,128)(2,1)}), bf16[2048,512]{1,0:T(8,128)(2,1)}) %all-gather.10.cloned.1.call-update) | async-done | bytes 2097168 | tf_op jit(solution)/shard_map/all_gather | solution.py:57
  66.1 5.2 %fusion.25 = bf16[1024,512]{1,0:T(8,128)(2,1)S(1)} fusion(bf16[2048,512]{1,0:T(8,128)(2,1)} %all-gather.10.cloned.1.call-done, bf16[1,1024,2048]{2,1,0:T(8,128)(2,1)} %param.9), kind=kOutput, calls=%fused_computation.32 | convolution fusion | flops 2148007936 | bytes 7340032 | tf_op jit(solution)/shard_map/dot_general | solution.py:53
  71.6 1.3 fusion.18
  76.7 72.3 %all-reduce = f32[64]{0:T(128)S(1)} all-reduce(f32[64]{0:T(128)S(1)} %dynamic-update-slice), channel_id=2, replica_groups=mesh['ctx'=32,'tp'=4,'fsdp'=2] {'ctx'}, use_global_device_ids=true, to_apply=%add | all-reduce | flops 64 | bytes 512
  149.1 5.0 %fusion.28 = f32[2,2,256,512]{3,2,1,0:T(8,128)} fusion(bf16[2,512,2,256]{1,3,2,0:T(8,128)(2,1)S(1)} %copy.69, f32[2,2,512]{2,1,0:T(2,128)S(1)} %reduce_window_sum.24, pred[512,512]{1,0:T(8,128)(4,1)S(1)} %iota_compare_fusion, bf16[2,512,2,256]{3,2,1,0:T(2,128)(2,1)} %copy-done.1, bf16[2,512,2,256]{3,1,0,2:T(8,128)(2,1)} %bitcast.79), kind=kOutput, calls=%fused_computation.33 | convolution fusion | flops 1078984704 | bytes 5513216 | tf_op jit(solution)/shard_map/chts,cshd->cthd/dot_general | solution.py:81
  154.1 59.7 %all-gather.16.cloned.1.call-done = f32[32,2,256,256]{3,2,1,0:T(8,128)} async-done(((f32[1,2,256,256]{3,2,1,0:T(8,128)}), f32[32,2,256,256]{3,2,1,0:T(8,128)}) %all-gather.16.cloned.1.call-update) | async-done | bytes 16777232 | tf_op jit(solution)/shard_map/all_gather | solution.py:12
  213.8 37.9 %while.14 = (s32[]{:T(128)}, f32[2,256,256]{2,1,0:T(8,128)S(1)}, s32[]{:T(128)}, f32[32,2]{1,0:T(8,128)S(1)}, f32[32,2,256,256]{3,2,1,0:T(8,128)}, /*index=5*/s32[]{:T(128)}, s32[]{:T(128)}) while((s32[]{:T(128)}, f32[2,256,256]{2,1,0:T(8,128)S(1)}, s32[]{:T(128)}, f32[32,2]{1,0:T(8,128)S(1)}, f32[32,2,256,256]{3,2,1,0:T(8,128)}, ...), condition=%wide.region_4.5_spmd.clone, body=%wide.region_3.4_spmd.clone.sunk | while | flops 524292 | bytes 1572993 | solution.py:21
  213.8 1.2 fusion.57
  215.0 1.2 fusion.57
  216.2 1.2 fusion.57
  217.5 1.2 fusion.57
  218.7 1.2 fusion.57
  219.9 1.2 fusion.57
  221.1 1.2 fusion.57
  222.3 1.2 fusion.57
  223.5 1.2 fusion.57
  224.7 1.2 fusion.57
  226.0 1.2 fusion.57
  227.3 1.2 fusion.57
  228.6 1.2 fusion.57
  229.8 1.2 fusion.57
  231.0 1.2 fusion.57
  232.2 1.2 fusion.57
  233.4 1.2 fusion.57
  234.6 1.2 fusion.57
  235.8 1.2 fusion.57
  241.9 1.2 fusion.57
  243.1 1.2 fusion.57
  244.4 1.2 fusion.57
  245.6 1.2 fusion.57
  253.0 3.6 fusion.49
  256.6 2.3 copy.73
  259.4 1.2 mul.152
  261.1 1.2 sub.45
  262.3 1.5 copy.79
  264.7 1.5 copy.78
  266.2 12.6 %fusion.36 = f32[1024,2048]{1,0:T(8,128)} fusion(bf16[512,2048]{1,0:T(8,128)(2,1)} %all-gather.18.cloned.1.call-done, f32[1024,512]{1,0:T(8,128)S(1)} %bitcast.83, f32[1024,512]{1,0:T(8,128)} %bitcast.85, f32[1024,512]{1,0:T(8,128)} %bitcast.84, bf16[2048,512]{1,0:T(8,128)(2,1)} %all-gather.8.cloned.1.call-done, bf16[1,1024,2048]{2,1,0:T(8,128)(2,1)} %param.9), kind=kOutput, calls=%fused_computation.44 | convolution fusion | flops 4300210176 | bytes 23068672 | tf_op jit(solution)/shard_map/dot_general | solution.py:114
  278.8 81.6 %reduce-scatter.2.cloned.1.call-done = f32[1024,512]{1,0:T(8,128)} async-done(((f32[1024,2048]{1,0:T(8,128)}), f32[1024,512]{1,0:T(8,128)}) %reduce-scatter.2.cloned.1.call-update) | async-done | bytes 2097168 | tf_op jit(solution)/shard_map/reduce_scatter | solution.py:119
  360.4 2.7 convert_bitcast_fusion
  (99 shorter events, 20.6 us)
Async XLA Ops:
  6.5 2.3 copy-start.4
  6.5 21.4 %all-gather.14.cloned.1.call-start = ((), (), s32[]{:S(2)}) async-start(), calls=%async_computation.4 | async-start | bytes 3145728 | tf_op jit(solution)/shard_map/all_gather | solution.py:56
  7.3 39.8 %all-gather.12.cloned.1.call-start = ((), (), s32[]{:S(2)}) async-start(), calls=%async_computation.3 | async-start | bytes 3145728 | tf_op jit(solution)/shard_map/all_gather | solution.py:55
  8.0 58.1 %all-gather.10.cloned.1.call-start = ((), (), s32[]{:S(2)}) async-start(), calls=%async_computation.2 | async-start | bytes 3145728 | tf_op jit(solution)/shard_map/all_gather | solution.py:57
  8.7 205.1 %all-gather.16.cloned.1.call-start = ((), (), s32[]{:S(2)}) async-start(), calls=%async_computation.5 | async-start | bytes 17301504 | tf_op jit(solution)/shard_map/all_gather | solution.py:12
  51.0 5.4 %copy-start.3 = (bf16[512,2048]{1,0:T(8,128)(2,1)S(1)}, bf16[512,2048]{1,0:T(8,128)(2,1)}, u32[]{:S(2)}) copy-start(bf16[512,2048]{1,0:T(8,128)(2,1)} %copy.63) | copy-start | bytes 6291460
  51.0 5.4 %copy-start.5 = (bf16[1,1024,2048]{2,1,0:T(8,128)(2,1)S(1)}, bf16[1,1024,2048]{2,1,0:T(8,128)(2,1)}, u32[]{:S(2)}) copy-start(bf16[1,1024,2048]{2,1,0:T(8,128)(2,1)} %param.9) | copy-start | bytes 12582916
  71.5 2.2 copy-start.1
  72.8 2.5 copy-start.6
  73.8 192.4 %all-gather.18.cloned.1.call-start = ((), (), s32[]{:S(2)}) async-start(), calls=%async_computation.6 | async-start | bytes 3145728 | tf_op jit(solution)/shard_map/all_gather | solution.py:116
  74.4 191.8 %all-gather.8.cloned.1.call-start = ((), (), s32[]{:S(2)}) async-start(), calls=%async_computation.1 | async-start | bytes 3145728 | tf_op jit(solution)/shard_map/all_gather | solution.py:58
  74.9 285.4 %reduce-scatter.2.cloned.1.call-start = ((), (), s32[]{:S(2)}) async-start(), calls=%async_computation.7 | async-start | bytes 10485760 | tf_op jit(solution)/shard_map/reduce_scatter | solution.py:119
  251.8 1.2 copy-start.2
  262.3 2.3 copy-start
Sparse Core Ops, SparseCore 0:
  9.1 18.8 all-gather.13
  29.8 17.1 all-gather.11
  48.8 17.1 all-gather.9
  73.9 139.8 all-gather.15
  215.4 14.1 all-gather.17
  231.3 17.1 all-gather.7
  278.9 81.4 reduce-scatter.1
where the time goes:
time: 373 us; the launch traced here: 370 us
  waiting for transfers between devices  179 us (48%)
  blocking collectives  72.3 us (19%)
  other arithmetic  46.6 us (12%)
  matrix products  35.3 us (9%)
  local copies, waits for them, and re-layouts  20.8 us (6%)
  between operations  14.3 us (4%)
    reduce_scatter x1, waiting for transfers between devices, on_device(): lax.psum_scatter(partial_terms, 'tp', scatter_dimension=1, tiled=True)  81.6 us
    unnamed x1, blocking collectives  72.3 us
    all_gather x1, waiting for transfers between devices, entering(): pieces = jax.tree.map(lambda part: lax.all_gather(part, axis), value)  59.7 us
    select_n x31, other arithmetic, hop(): jnp.where(position < mine, new, old)  36.7 us
    all_gather x1, waiting for transfers between devices, on_device(): lax.all_gather(query_weight, 'fsdp', axis=0, tiled=True)  15.1 us
    all_gather x1, waiting for transfers between devices, on_device(): key_proj = add_rows(lax.all_gather(key_weight, 'fsdp', axis=0, tiled=True))  14.7 us
    dot_general x3, matrix products, add_rows(): return jnp.dot(token_rows, shard_rows, preferred_element_type=jnp.float32)  12.9 us
    dot_general x1, matrix products, on_device(): jnp.dot(hidden, lax.all_gather(out_weight, 'fsdp', axis=1, tiled=True), p...  12.6 us
  transfers between devices with their start and end apart: 7, of which 5 were waited for; matrix products, arithmetic and copies ran while one was open for 21% of the time, Pallas kernels for 0%

commit v1 on v0

v1 whole, which is shorter than its diff:
```python
import jax
import jax.numpy as jnp
import numpy as np
from jax import lax
from jax.experimental import pallas as pl
from jax.experimental.pallas import tpu as pltpu
from jax.sharding import PartitionSpec as P

DH = 256
HALF = DH // 2
BLOCK = 512
KEY, VALUE, QUERY, GATE = range(4)
F32, BF16 = jnp.float32, jnp.bfloat16


def dot(a, b):
    return jnp.dot(a, b, preferred_element_type=F32)


def rotation_rows(ctx_count, rows):
    frequency = 10000.0 ** (-np.arange(HALF) / HALF)
    tables = []
    for stride, count in ((32, rows // 32), (1, 32), (rows, ctx_count)):
        angles = (np.arange(count) * stride)[:, None] * frequency[None, :]
        tables += [np.cos(angles), np.sin(angles)]
    return [t.astype(np.float32) for t in tables]


def make_kernel(n_ctx, n_tp):
    n_peers = n_ctx - 1

    def kernel(
        tok, wk, wv, wq, wg, wo, ld, cos_a, sin_a, cos_b, sin_b, cos_c, sin_c, out,
        tokv, wown, woth, wov, acc, kb, vb, qb, gb, ret, ust, ubuf, rbuf, pbuf, sbuf,
        abuf, arcv, crow, ccol, cosv, sinv, hid, oacc, obuf,
        tsem, lsem, wsend, wrecv, asend, arecv, usend, urecv, psend, precv,
        wolocal, wosend, worecv, wofwd, agsend, agrecv, fwsend, fwrecv, osem,
    ):
        ctx, tp, core = (lax.axis_index(n) for n in ("ctx", "tp", "fsdp"))
        rows = tok.shape[0]
        khalf = tok.shape[1] // 2
        partner = {"fsdp": 1 - core}
        right = {"tp": lax.rem(tp + 1, n_tp)}
        left = {"tp": lax.rem(tp + n_tp - 1, n_tp)}
        weights = (wk, wv, wq, wg)

        barrier = pltpu.get_barrier_semaphore()
        pl.semaphore_signal(barrier, inc=1, device_id=partner)
        for k in range(1, n_tp):
            pl.semaphore_signal(barrier, inc=1, device_id={"tp": lax.rem(tp + k, n_tp)})

        def greet(k, carry):
            pl.semaphore_signal(barrier, inc=1, device_id={"ctx": lax.rem(ctx + k, n_ctx)})
            return carry

        lax.fori_loop(1, n_ctx, greet, 0)

        def tok_copy(part):
            half = core if part == 0 else 1 - core
            columns = pl.ds(pl.multiple_of(half * khalf, khalf), khalf)
            return pltpu.make_async_copy(tok.at[:, columns], tokv.at[part], tsem.at[part])

        def own_copy(i, h):
            source = weights[i].at[:, h * DH : (h + 1) * DH]
            return pltpu.make_async_copy(source, wown.at[i, h], lsem.at[i, h])

        order = [(KEY, 0), (VALUE, 0), (KEY, 1), (VALUE, 1), (QUERY, 0), (GATE, 0), (QUERY, 1), (GATE, 1)]
        tok_copy(0).start()
        for i, h in order[:2]:
            own_copy(i, h).start()
        tok_copy(1).start()
        for i, h in order[2:]:
            own_copy(i, h).start()

        crow[...] = jnp.zeros_like(crow)
        crow[0 : ld.shape[0], :] = ld[...]
        running = crow[...]
        lane = lax.rem(lax.broadcasted_iota(jnp.int32, running.shape, 1), BLOCK)
        step = 1
        while step < BLOCK:
            running = running + jnp.where(lane >= step, pltpu.roll(running, step, 1), 0.0)
            step *= 2
        crow[...] = running
        ccol[...] = running.T
        ends = [crow[:, (b + 1) * BLOCK - 1 : (b + 1) * BLOCK] for b in range(2)]
        total = ends[0] + ends[1]
        abuf[...] = jnp.broadcast_to(total, abuf.shape)
        arcv[ctx] = jnp.broadcast_to(total, abuf.shape)

        cc, sc = cos_c[pl.ds(ctx, 1), :], sin_c[pl.ds(ctx, 1), :]
        cosv[0:32, :] = cos_a[...] * cc - sin_a[...] * sc
        sinv[0:32, :] = sin_a[...] * cc + cos_a[...] * sc
        base_cos, base_sin = cosv[0:32, :], sinv[0:32, :]
        for a in range(rows // 32):
            ca, sa = base_cos[a : a + 1, :], base_sin[a : a + 1, :]
            cosv[a * 32 : (a + 1) * 32, :] = ca * cos_b[...] - sa * sin_b[...]
            sinv[a * 32 : (a + 1) * 32, :] = sa * cos_b[...] + ca * sin_b[...]

        def own_product(i, h):
            own_copy(i, h).wait()
            acc[i, h] = dot(tokv[0], wown[i, h])

        tok_copy(0).wait()
        own_product(KEY, 0)
        own_product(VALUE, 0)

        pl.semaphore_wait(barrier, 1 + (n_tp - 1) + n_peers)

        def swap(i, h):
            return pltpu.make_async_remote_copy(
                src_ref=weights[i].at[:, h * DH : (h + 1) * DH],
                dst_ref=woth.at[i, h],
                send_sem=wsend.at[i, h],
                recv_sem=wrecv.at[i, h],
                device_id=partner,
            )

        for i, h in order:
            swap(i, h).start()

        def send_total(k, carry):
            pltpu.make_async_remote_copy(
                src_ref=abuf,
                dst_ref=arcv.at[ctx],
                send_sem=asend,
                recv_sem=arecv,
                device_id={"ctx": lax.rem(ctx + k, n_ctx)},
            ).start()
            return carry

        lax.fori_loop(1, n_ctx, send_total, 0)

        per_core = n_tp // 2
        width = wo.shape[1] // per_core

        def wo_send(j):
            return pltpu.make_async_remote_copy(
                src_ref=wo.at[:, j * width : (j + 1) * width],
                dst_ref=wov.at[tp],
                send_sem=wosend.at[j],
                recv_sem=worecv.at[tp],
                device_id={"tp": per_core * core + j},
            )

        def wo_own(j):
            return pltpu.make_async_copy(
                wo.at[:, j * width : (j + 1) * width], wov.at[tp], wolocal
            )

        def wo_from(r):
            return pltpu.make_async_remote_copy(
                src_ref=wov.at[r],
                dst_ref=wov.at[r],
                send_sem=wofwd.at[r],
                recv_sem=worecv.at[r],
                device_id=partner,
            )

        for j in range(per_core):
            here = per_core * core + j == tp

            @pl.when(jnp.logical_not(here))
            def _():
                wo_send(j).start()

            @pl.when(here)
            def _():
                wo_own(j).start()

        def positions(b):
            return slice(b * BLOCK, (b + 1) * BLOCK)

        def project(i, h):
            swap(i, h).wait_recv()
            return acc[i, h] + dot(tokv[1], woth[i, h])

        def rotated(u):
            first, second = u[:, :HALF], u[:, HALF:]
            cosine, sine = cosv[...], sinv[...]
            return (first * cosine - second * sine).astype(BF16), (
                second * cosine + first * sine
            ).astype(BF16)

        def key_value(h):
            kb[h, :, :HALF], kb[h, :, HALF:] = rotated(project(KEY, h))
            vb[h] = project(VALUE, h).astype(BF16)

        def query_gate(h):
            qb[h, :, :HALF], qb[h, :, HALF:] = rotated(project(QUERY, h))
            gb[h] = project(GATE, h).astype(BF16)

        def block_end(h, b):
            return crow[h : h + 1, (b + 1) * BLOCK - 1 : (b + 1) * BLOCK]

        def decay_column(h, b):
            return ccol[positions(b), h : h + 1]

        def states(h):
            for b in range(2):
                scale = jnp.exp(block_end(h, b) - decay_column(h, b))
                scaled = (kb[h, positions(b)].astype(F32) * scale).astype(BF16)
                ust[h, b] = lax.dot_general(
                    scaled, vb[h, positions(b)], (((0,), (0,)), ((), ())),
                    preferred_element_type=F32,
                )
            joined = (jnp.exp(block_end(h, 1)) * ust[h, 0] + ust[h, 1]).astype(BF16)
            for j in range(2):
                ubuf[h, j * 16 : (j + 1) * 16] = joined[:, j * HALF : (j + 1) * HALF].reshape(16, 16, HALF)
            rbuf[h, ctx] = ubuf[h, ctx]

            def send(k, carry):
                to = lax.rem(ctx + k, n_ctx)
                pltpu.make_async_remote_copy(
                    src_ref=ubuf.at[h, to],
                    dst_ref=rbuf.at[h, ctx],
                    send_sem=usend.at[h],
                    recv_sem=urecv.at[h],
                    device_id={"ctx": to},
                ).start()
                return carry

            lax.fori_loop(1, n_ctx, send, 0)

        def many(buffer, send_sem, recv_sem):
            part = buffer.at[pl.ds(0, n_peers)]
            return pltpu.make_async_remote_copy(
                src_ref=part, dst_ref=part, send_sem=send_sem, recv_sem=recv_sem,
                device_id={"ctx": lax.rem(ctx + 1, n_ctx)},
            )

        def scan(h):
            many(rbuf.at[h], usend.at[h], urecv.at[h]).wait_recv()

            def hop(d, before):
                pbuf[h, d] = before.astype(BF16)
                return before * jnp.exp(arcv[d, h : h + 1, :]) + rbuf[h, d].astype(F32)

            lax.fori_loop(0, n_ctx, hop, jnp.zeros((16, HALF), F32))
            sbuf[h, ctx] = pbuf[h, ctx]

            def send(k, carry):
                to = lax.rem(ctx + k, n_ctx)
                pltpu.make_async_remote_copy(
                    src_ref=pbuf.at[h, to],
                    dst_ref=sbuf.at[h, ctx],
                    send_sem=psend.at[h],
                    recv_sem=precv.at[h],
                    device_id={"ctx": to},
                ).start()
                return carry

            lax.fori_loop(1, n_ctx, send, 0)

        quarter = BLOCK // 2

        def intra(h):
            for b in range(2):
                for part in range(2):
                    start = b * BLOCK + part * quarter
                    extent = (part + 1) * quarter
                    mine = slice(start, start + quarter)
                    seen = slice(b * BLOCK, b * BLOCK + extent)
                    scores = lax.dot_general(
                        qb[h, mine], kb[h, seen], (((1,), (1,)), ((), ())),
                        preferred_element_type=F32,
                    )
                    t = lax.broadcasted_iota(jnp.int32, scores.shape, 0) + part * quarter
                    s = lax.broadcasted_iota(jnp.int32, scores.shape, 1)
                    differ = ccol[mine, h : h + 1] - crow[h : h + 1, seen]
                    decay = jnp.exp(jnp.where(t >= s, differ, 0.0))
                    mixed = jnp.where(t >= s, scores * decay, 0.0).astype(BF16)
                    ret[h, mine] = dot(mixed, vb[h, seen])

        def ag_own(h, b, way):
            return pltpu.make_async_remote_copy(
                src_ref=hid.at[tp, h, b],
                dst_ref=hid.at[tp, h, b],
                send_sem=agsend.at[way, h, b],
                recv_sem=agrecv.at[way, h, b],
                device_id=right if way == 0 else left,
            )

        def ag_forward(h, way):
            source = lax.rem(tp + (n_tp - 1 if way == 0 else 1), n_tp)
            return pltpu.make_async_remote_copy(
                src_ref=hid.at[source, h, way],
                dst_ref=hid.at[source, h, way],
                send_sem=fwsend.at[way, h],
                recv_sem=fwrecv.at[way, h],
                device_id=right if way == 0 else left,
            )

        def finish(h):
            many(sbuf.at[h], psend.at[h], precv.at[h]).wait_recv()
            state = jnp.concatenate(
                [sbuf[h, j * 16 : (j + 1) * 16].reshape(DH, HALF) for j in range(2)], axis=1
            )
            later = (jnp.exp(block_end(h, 0)) * state.astype(F32) + ust[h, 0]).astype(BF16)
            for b in range(2):
                prior = state if b == 0 else later
                inter = jnp.exp(decay_column(h, b)) * dot(qb[h, positions(b)], prior)
                retained = ret[h, positions(b)] + inter
                center = retained - jnp.mean(retained, axis=-1, keepdims=True)
                spread = jnp.mean(center * center, axis=-1, keepdims=True)
                normed = center * lax.rsqrt(spread + 1e-5)
                gates = gb[h, positions(b)].astype(F32)
                silu = gates / (1.0 + jnp.exp(-gates))
                hid[tp, h, b] = (silu * normed).astype(BF16)
                for way in range(2):
                    ag_own(h, b, way).start()

        def fold(source, h, b, first=False):
            product = dot(hid[source, h, b], wov[source, h * DH : (h + 1) * DH, :])
            oacc[b] = product if first else oacc[b] + product

        for i, h in order[2:4]:
            own_product(i, h)
        tok_copy(1).wait()
        key_value(0)
        states(0)
        key_value(1)
        states(1)

        own_product(QUERY, 0)
        own_product(GATE, 0)
        query_gate(0)
        many(arcv, asend, arecv).wait_recv()
        scan(0)
        intra(0)
        own_product(QUERY, 1)
        own_product(GATE, 1)
        query_gate(1)
        scan(1)

        holder = tp // per_core == core
        for j in range(per_core):
            @pl.when(per_core * core + j == tp)
            def _():
                wo_own(j).wait()

        @pl.when(holder)
        def _():
            wo_from(tp).start()

        for k in range(1, n_tp):
            r = lax.rem(tp + k, n_tp)

            @pl.when(holder)
            def _():
                wo_from(r).wait_recv()
                wo_from(r).start()

        intra(1)
        finish(0)
        finish(1)

        @pl.when(jnp.logical_not(holder))
        def _():
            for r in range(n_tp):
                wo_from(r).wait_recv()

        @pl.when(holder)
        def _():
            for r in range(n_tp):
                wo_from(r).wait_send()

        for j in range(per_core):
            @pl.when(per_core * core + j != tp)
            def _():
                wo_send(j).wait_send()

        for h in range(2):
            for b in range(2):
                fold(tp, h, b, first=h == 0)
        before, after = lax.rem(tp + n_tp - 1, n_tp), lax.rem(tp + 1, n_tp)
        opposite = lax.rem(tp + 2, n_tp)
        for h in range(2):
            for b in range(2):
                ag_own(h, b, 0).wait_recv()
                if b == 0:
                    ag_forward(h, 0).start()
                ag_own(h, b, 1).wait_recv()
                if b == 1:
                    ag_forward(h, 1).start()
                fold(before, h, b)
                fold(after, h, b)
        for h in range(2):
            for way in range(2):
                ag_forward(h, way).wait_recv()
                fold(opposite, h, way)
                if h == 1:
                    obuf[positions(way)] = oacc[way].astype(BF16)
                    pltpu.make_async_copy(
                        obuf.at[positions(way)], out.at[positions(way)], osem.at[way]
                    ).start()

        for i, h in order:
            swap(i, h).wait_send()
        many(arcv, asend, arecv).wait_send()
        for h in range(2):
            many(rbuf.at[h], usend.at[h], urecv.at[h]).wait_send()
            many(sbuf.at[h], psend.at[h], precv.at[h]).wait_send()
            for way in range(2):
                for b in range(2):
                    ag_own(h, b, way).wait_send()
                ag_forward(h, way).wait_send()
        for way in range(2):
            pltpu.make_async_copy(
                obuf.at[positions(way)], out.at[positions(way)], osem.at[way]
            ).wait()

    return kernel


def solution(mesh):
    n_ctx, n_tp = mesh.shape["ctx"], mesh.shape["tp"]

    def on_device(tokens, query_weight, key_weight, value_weight, gate_weight, out_weight, log_decay):
        rows, depth = tokens.shape[1:]
        cols = query_weight.shape[1]
        out_rows = out_weight.shape[0]
        tables = rotation_rows(n_ctx, rows)
        vmem = lambda *shape, dtype=BF16: pltpu.VMEM(shape, dtype)
        dma = lambda *shape: pltpu.SemaphoreType.DMA(shape)
        anywhere = pl.BlockSpec(memory_space=pl.ANY)
        small = pl.BlockSpec(memory_space=pltpu.VMEM)
        result = pl.pallas_call(
            make_kernel(n_ctx, n_tp),
            out_shape=jax.ShapeDtypeStruct((rows, cols), BF16),
            in_specs=[anywhere] * 6 + [small] * 7,
            out_specs=anywhere,
            scratch_shapes=[
                vmem(2, rows, depth // 2),
                vmem(4, 2, depth // 2, DH),
                vmem(4, 2, depth // 2, DH),
                vmem(n_tp, out_rows, cols),
                vmem(4, 2, rows, DH, dtype=F32),
                vmem(2, rows, DH),
                vmem(2, rows, DH),
                vmem(2, rows, DH),
                vmem(2, rows, DH),
                vmem(2, rows, DH, dtype=F32),
                vmem(2, 2, DH, DH, dtype=F32),
                vmem(2, n_ctx, 16, HALF),
                vmem(2, n_ctx, 16, HALF),
                vmem(2, n_ctx, 16, HALF),
                vmem(2, n_ctx, 16, HALF),
                vmem(8, HALF, dtype=F32),
                vmem(n_ctx, 8, HALF, dtype=F32),
                vmem(8, rows, dtype=F32),
                vmem(rows, 8, dtype=F32),
                vmem(rows, HALF, dtype=F32),
                vmem(rows, HALF, dtype=F32),
                vmem(n_tp, 2, 2, BLOCK, DH),
                vmem(2, BLOCK, cols, dtype=F32),
                vmem(rows, cols),
                dma(2), dma(4, 2), dma(4, 2), dma(4, 2), dma(), dma(),
                dma(2), dma(2), dma(2), dma(2),
                dma(), dma(2), dma(n_tp), dma(n_tp),
                dma(2, 2, 2), dma(2, 2, 2), dma(2, 2), dma(2, 2), dma(2),
            ],
            compiler_params=pltpu.CompilerParams(
                collective_id=0, has_side_effects=True, vmem_limit_bytes=60 << 20
            ),
            name="retention",
        )(
            tokens[0], key_weight, value_weight, query_weight, gate_weight, out_weight,
            jnp.transpose(log_decay[0]), *tables,
        )
        return result[None]

    in_specs = (
        P("fsdp", "ctx", None),
        P("fsdp", "tp"),
        P("fsdp", "tp"),
        P("fsdp", "tp"),
        P("fsdp", "tp"),
        P("tp", "fsdp"),
        P("fsdp", "ctx", "tp"),
    )
    out_specs = P("fsdp", "ctx", "tp")
    return jax.shard_map(
        on_device, mesh=mesh, in_specs=in_specs, out_specs=out_specs, check_vma=False
    )
```

time: 373 us -> 74.4 us (0.20)
  waiting for transfers between devices: 179 us -> 0 us
  blocking collectives: 72.3 us -> 0 us
  Pallas kernels: 0 us -> 71.4 us
  other arithmetic: 46.6 us -> 0 us
  matrix products: 35.3 us -> 0 us
  local copies, waits for them, and re-layouts: 20.8 us -> 2.26 us
  between operations: 14.3 us -> 0.01 us
    all_gather x6 -> x0, waiting for transfers between devices: 94.4 us -> none  [the longest x1 59.7 us: entering(): pieces = jax.tree.map(lambda part: lax.all_gather(part, axis), value)]
    reduce_scatter x1 -> x0, waiting for transfers between devices: 81.6 us -> none  [on_device(): lax.psum_scatter(partial_terms, 'tp', scatter_dimension=1, tiled=True)]
    unnamed x1 -> x0, blocking collectives: 72.3 us -> none
    pallas_call x0 -> x1, Pallas kernels: none -> 71.4 us  [on_device(): pl.pallas_call(make_kernel(n_ctx, n_tp), out_shape=jax.ShapeDtypeStruct((...]
    select_n x31 -> x0, other arithmetic: 36.7 us -> none  [hop(): jnp.where(position < mine, new, old)]
    dot_general x7 -> x0, matrix products: 35.3 us -> none  [the longest x3 12.9 us: add_rows(): return jnp.dot(token_rows, shard_rows, preferred_element_type=jnp.float32)]
    dot_general x2 -> x0, local copies, waits for them, and re-layouts: 7.95 us -> none  [add_rows(): return jnp.dot(token_rows, shard_rows, preferred_element_type=jnp.float32)]
  transfers between devices with their start and end apart: 7 -> 0, of which waited for: 5 -> 0; matrix products, arithmetic and copies ran while one was open for 21% -> 0% of each run, Pallas kernels for 0% -> 0%
where the time goes in v1:
time: 74.4 us; the launch traced here: 73.6 us
  Pallas kernels  71.4 us (96%)
  local copies, waits for them, and re-layouts  2.26 us (3%)
    pallas_call x1, Pallas kernels, on_device(): pl.pallas_call(make_kernel(n_ctx, n_tp), out_shape=jax.ShapeDtypeStruct((...  71.4 us
    unnamed x1, local copies, waits for them, and re-layouts  2.26 us

profile of v1, /device:TPU:8, one launch (start us, length us, event | category | flops | bytes accessed | tf_op | source)
XLA Modules:
  0.0 73.6 jit_solution(17813789936655445803)
XLA Ops:
  0.0 71.4 %retention.1 = bf16[1024,512]{1,0:T(8,128)(2,1)} custom-call(bf16[1024,2048]{1,0:T(8,128)(2,1)} %bitcast.6, bf16[1024,512]{1,0:T(8,128)(2,1)} %wk.1, bf16[1024,512]{1,0:T(8,128)(2,1)} %wv.1, bf16[1024,512]{1,0:T(8,128)(2,1)} %wq.1, bf16[1024,512]{1,0:T(8,128)(2,1)} %wg.1, bf16[512,1024]{1,0:T(8,128)(2,1)} %wo.1, f32[2,1024]{1,0:T(2,128)} %bitcast.7, ...), custom_call_target="tpu_custom_call" | custom-call | tf_op jit(solution)/shard_map/retention/pallas_call | solution.py:427
  71.4 2.3 %copy.15 = bf16[1,1024,512]{2,1,0:T(8,128)(2,1)} copy(bf16[1,1024,512]{2,1,0:T(8,128)(2,1)} %bitcast.5) | data formatting | bytes 2097152

commit v2 on v1

--- a/solution.py
+++ b/solution.py
@@ -31,7 +31,7 @@
 
     def kernel(
         tok, wk, wv, wq, wg, wo, ld, cos_a, sin_a, cos_b, sin_b, cos_c, sin_c, out,
-        tokv, wown, woth, wov, acc, kb, vb, qb, gb, ret, ust, ubuf, rbuf, pbuf, sbuf,
+        tokv, wv_all, wov, acc, kb, vb, qb, gb, ret, ust, ubuf, rbuf, pbuf, sbuf,
         abuf, arcv, crow, ccol, cosv, sinv, hid, oacc, obuf,
         tsem, lsem, wsend, wrecv, asend, arecv, usend, urecv, psend, precv,
         wolocal, wosend, worecv, wofwd, agsend, agrecv, fwsend, fwrecv, osem,
@@ -55,16 +55,18 @@
 
         lax.fori_loop(1, n_ctx, greet, 0)
 
+        own_rows = pl.ds(pl.multiple_of(core * khalf, khalf), khalf)
+        other_rows = pl.ds(pl.multiple_of((1 - core) * khalf, khalf), khalf)
+
         def tok_copy(part):
-            half = core if part == 0 else 1 - core
-            columns = pl.ds(pl.multiple_of(half * khalf, khalf), khalf)
-            return pltpu.make_async_copy(tok.at[:, columns], tokv.at[part], tsem.at[part])
+            columns = own_rows if part == 0 else other_rows
+            return pltpu.make_async_copy(tok.at[:, columns], tokv.at[:, columns], tsem.at[part])
 
         def own_copy(i, h):
             source = weights[i].at[:, h * DH : (h + 1) * DH]
-            return pltpu.make_async_copy(source, wown.at[i, h], lsem.at[i, h])
-
-        order = [(KEY, 0), (VALUE, 0), (KEY, 1), (VALUE, 1), (QUERY, 0), (GATE, 0), (QUERY, 1), (GATE, 1)]
+            return pltpu.make_async_copy(source, wv_all.at[i, h, own_rows], lsem.at[i, h])
+
+        order = [(KEY, 0), (VALUE, 0), (QUERY, 0), (GATE, 0), (KEY, 1), (VALUE, 1), (QUERY, 1), (GATE, 1)]
         tok_copy(0).start()
         for i, h in order[:2]:
             own_copy(i, h).start()
@@ -87,29 +89,12 @@
         abuf[...] = jnp.broadcast_to(total, abuf.shape)
         arcv[ctx] = jnp.broadcast_to(total, abuf.shape)
 
-        cc, sc = cos_c[pl.ds(ctx, 1), :], sin_c[pl.ds(ctx, 1), :]
-        cosv[0:32, :] = cos_a[...] * cc - sin_a[...] * sc
-        sinv[0:32, :] = sin_a[...] * cc + cos_a[...] * sc
-        base_cos, base_sin = cosv[0:32, :], sinv[0:32, :]
-        for a in range(rows // 32):
-            ca, sa = base_cos[a : a + 1, :], base_sin[a : a + 1, :]
-            cosv[a * 32 : (a + 1) * 32, :] = ca * cos_b[...] - sa * sin_b[...]
-            sinv[a * 32 : (a + 1) * 32, :] = sa * cos_b[...] + ca * sin_b[...]
-
-        def own_product(i, h):
-            own_copy(i, h).wait()
-            acc[i, h] = dot(tokv[0], wown[i, h])
-
-        tok_copy(0).wait()
-        own_product(KEY, 0)
-        own_product(VALUE, 0)
-
         pl.semaphore_wait(barrier, 1 + (n_tp - 1) + n_peers)
 
         def swap(i, h):
             return pltpu.make_async_remote_copy(
                 src_ref=weights[i].at[:, h * DH : (h + 1) * DH],
-                dst_ref=woth.at[i, h],
+                dst_ref=wv_all.at[i, h, own_rows],
                 send_sem=wsend.at[i, h],
                 recv_sem=wrecv.at[i, h],
                 device_id=partner,
@@ -167,12 +152,29 @@
             def _():
                 wo_own(j).start()
 
+        cc, sc = cos_c[pl.ds(ctx, 1), :], sin_c[pl.ds(ctx, 1), :]
+        cosv[0:32, :] = cos_a[...] * cc - sin_a[...] * sc
+        sinv[0:32, :] = sin_a[...] * cc + cos_a[...] * sc
+        base_cos, base_sin = cosv[0:32, :], sinv[0:32, :]
+        for a in range(rows // 32):
+            ca, sa = base_cos[a : a + 1, :], base_sin[a : a + 1, :]
+            cosv[a * 32 : (a + 1) * 32, :] = ca * cos_b[...] - sa * sin_b[...]
+            sinv[a * 32 : (a + 1) * 32, :] = sa * cos_b[...] + ca * sin_b[...]
+
         def positions(b):
             return slice(b * BLOCK, (b + 1) * BLOCK)
 
-        def project(i, h):
+        def own_product(i, h):
+            own_copy(i, h).wait()
+            acc[i] = dot(tokv[:, own_rows], wv_all[i, h, own_rows])
+
+        def project(i, h, split=False):
+            if split:
+                swap(i, h).wait_recv()
+                return acc[i] + dot(tokv[:, other_rows], wv_all[i, h, other_rows])
+            own_copy(i, h).wait()
             swap(i, h).wait_recv()
-            return acc[i, h] + dot(tokv[1], woth[i, h])
+            return dot(tokv[...], wv_all[i, h])
 
         def rotated(u):
             first, second = u[:, :HALF], u[:, HALF:]
@@ -182,8 +184,9 @@
             ).astype(BF16)
 
         def key_value(h):
-            kb[h, :, :HALF], kb[h, :, HALF:] = rotated(project(KEY, h))
-            vb[h] = project(VALUE, h).astype(BF16)
+            split = h == 0
+            kb[h, :, :HALF], kb[h, :, HALF:] = rotated(project(KEY, h, split))
+            vb[h] = project(VALUE, h, split).astype(BF16)
 
         def query_gate(h):
             qb[h, :, :HALF], qb[h, :, HALF:] = rotated(project(QUERY, h))
@@ -306,31 +309,28 @@
                 gates = gb[h, positions(b)].astype(F32)
                 silu = gates / (1.0 + jnp.exp(-gates))
                 hid[tp, h, b] = (silu * normed).astype(BF16)
-                for way in range(2):
-                    ag_own(h, b, way).start()
+                ag_own(h, b, b).start()
+            ag_own(h, 1, 0).start()
+            ag_own(h, 0, 1).start()
 
         def fold(source, h, b, first=False):
             product = dot(hid[source, h, b], wov[source, h * DH : (h + 1) * DH, :])
             oacc[b] = product if first else oacc[b] + product
 
-        for i, h in order[2:4]:
-            own_product(i, h)
+        tok_copy(0).wait()
+        own_product(KEY, 0)
+        own_product(VALUE, 0)
         tok_copy(1).wait()
         key_value(0)
         states(0)
+        query_gate(0)
+        intra(0)
+        many(arcv, asend, arecv).wait_recv()
+        scan(0)
         key_value(1)
         states(1)
-
-        own_product(QUERY, 0)
-        own_product(GATE, 0)
-        query_gate(0)
-        many(arcv, asend, arecv).wait_recv()
-        scan(0)
-        intra(0)
-        own_product(QUERY, 1)
-        own_product(GATE, 1)
         query_gate(1)
-        scan(1)
+        finish(0)
 
         holder = tp // per_core == core
         for j in range(per_core):
@@ -351,40 +351,36 @@
                 wo_from(r).start()
 
         intra(1)
-        finish(0)
-        finish(1)
+        scan(1)
 
         @pl.when(jnp.logical_not(holder))
         def _():
             for r in range(n_tp):
                 wo_from(r).wait_recv()
 
-        @pl.when(holder)
-        def _():
-            for r in range(n_tp):
-                wo_from(r).wait_send()
-
-        for j in range(per_core):
-            @pl.when(per_core * core + j != tp)
-            def _():
-                wo_send(j).wait_send()
-
-        for h in range(2):
-            for b in range(2):
-                fold(tp, h, b, first=h == 0)
         before, after = lax.rem(tp + n_tp - 1, n_tp), lax.rem(tp + 1, n_tp)
         opposite = lax.rem(tp + 2, n_tp)
+
+        def neighbours(h):
+            for way in range(2):
+                ag_own(h, way, way).wait_recv()
+                ag_forward(h, way).start()
+            fold(before, h, 0)
+            fold(after, h, 1)
+
+        for b in range(2):
+            fold(tp, 0, b, first=True)
+        neighbours(0)
+        finish(1)
+        for b in range(2):
+            fold(tp, 1, b)
         for h in range(2):
-            for b in range(2):
-                ag_own(h, b, 0).wait_recv()
-                if b == 0:
-                    ag_forward(h, 0).start()
-                ag_own(h, b, 1).wait_recv()
-                if b == 1:
-                    ag_forward(h, 1).start()
-                fold(before, h, b)
-                fold(after, h, b)
-        for h in range(2):
+            if h == 1:
+                neighbours(h)
+            ag_own(h, 1, 0).wait_recv()
+            fold(before, h, 1)
+            ag_own(h, 0, 1).wait_recv()
+            fold(after, h, 0)
             for way in range(2):
                 ag_forward(h, way).wait_recv()
                 fold(opposite, h, way)
@@ -393,6 +389,16 @@
                     pltpu.make_async_copy(
                         obuf.at[positions(way)], out.at[positions(way)], osem.at[way]
                     ).start()
+
+        @pl.when(holder)
+        def _():
+            for r in range(n_tp):
+                wo_from(r).wait_send()
+
+        for j in range(per_core):
+            @pl.when(per_core * core + j != tp)
+            def _():
+                wo_send(j).wait_send()
 
         for i, h in order:
             swap(i, h).wait_send()
@@ -430,11 +436,10 @@
             in_specs=[anywhere] * 6 + [small] * 7,
             out_specs=anywhere,
             scratch_shapes=[
-                vmem(2, rows, depth // 2),
-                vmem(4, 2, depth // 2, DH),
-                vmem(4, 2, depth // 2, DH),
+                vmem(rows, depth),
+                vmem(4, 2, depth, DH),
                 vmem(n_tp, out_rows, cols),
-                vmem(4, 2, rows, DH, dtype=F32),
+                vmem(2, rows, DH, dtype=F32),
                 vmem(2, rows, DH),
                 vmem(2, rows, DH),
                 vmem(2, rows, DH),

time: 74.4 us -> 73.9 us (level)
  Pallas kernels: 71.4 us -> 70.5 us
    pallas_call x1, Pallas kernels: 71.4 us -> 70.5 us  [on_device(): pl.pallas_call(make_kernel(n_ctx, n_tp), out_shape=jax.ShapeDtypeStruct((...]
where the time goes in v2:
time: 73.9 us; the launch traced here: 72.8 us
  Pallas kernels  70.5 us (95%)
  local copies, waits for them, and re-layouts  2.26 us (3%)
    pallas_call x1, Pallas kernels, on_device(): pl.pallas_call(make_kernel(n_ctx, n_tp), out_shape=jax.ShapeDtypeStruct((...  70.5 us
    unnamed x1, local copies, waits for them, and re-layouts  2.26 us

profile of v2, /device:TPU:8, one launch (start us, length us, event | category | flops | bytes accessed | tf_op | source)
XLA Modules:
  0.0 72.8 jit_solution(17638884559031794245)
XLA Ops:
  0.0 70.5 %retention.1 = bf16[1024,512]{1,0:T(8,128)(2,1)} custom-call(bf16[1024,2048]{1,0:T(8,128)(2,1)} %bitcast.6, bf16[1024,512]{1,0:T(8,128)(2,1)} %wk.1, bf16[1024,512]{1,0:T(8,128)(2,1)} %wv.1, bf16[1024,512]{1,0:T(8,128)(2,1)} %wq.1, bf16[1024,512]{1,0:T(8,128)(2,1)} %wg.1, bf16[512,1024]{1,0:T(8,128)(2,1)} %wo.1, f32[2,1024]{1,0:T(2,128)} %bitcast.7, ...), custom_call_target="tpu_custom_call" | custom-call | tf_op jit(solution)/shard_map/retention/pallas_call | solution.py:433
  70.5 2.3 %copy.15 = bf16[1,1024,512]{2,1,0:T(8,128)(2,1)} copy(bf16[1,1024,512]{2,1,0:T(8,128)(2,1)} %bitcast.5) | data formatting | bytes 2097152

commit v3 on v2

--- a/solution.py
+++ b/solution.py
@@ -9,6 +9,8 @@
 DH = 256
 HALF = DH // 2
 BLOCK = 512
+PIECES = 4
+PIECE = BLOCK // PIECES
 KEY, VALUE, QUERY, GATE = range(4)
 F32, BF16 = jnp.float32, jnp.bfloat16
 
@@ -32,22 +34,25 @@
     def kernel(
         tok, wk, wv, wq, wg, wo, ld, cos_a, sin_a, cos_b, sin_b, cos_c, sin_c, out,
         tokv, wv_all, wov, acc, kb, vb, qb, gb, ret, ust, ubuf, rbuf, pbuf, sbuf,
-        abuf, arcv, crow, ccol, cosv, sinv, hid, oacc, obuf,
+        abuf, arcv, crow, ccol, cosv, sinv, stv, hid, away, oacc, obuf,
         tsem, lsem, wsend, wrecv, asend, arecv, usend, urecv, psend, precv,
-        wolocal, wosend, worecv, wofwd, agsend, agrecv, fwsend, fwrecv, osem,
+        wolocal, wosend, worecv, wofwd, wogot, crsend, crrecv, mtsend, mtrecv,
+        fwsend, fwrecv, p2send, p2recv, osem,
     ):
         ctx, tp, core = (lax.axis_index(n) for n in ("ctx", "tp", "fsdp"))
         rows = tok.shape[0]
         khalf = tok.shape[1] // 2
         partner = {"fsdp": 1 - core}
-        right = {"tp": lax.rem(tp + 1, n_tp)}
-        left = {"tp": lax.rem(tp + n_tp - 1, n_tp)}
+        mate_tp, cross_tp = tp + 1 - 2 * lax.rem(tp, 2), n_tp - 1 - tp
+        opposite_tp = lax.rem(tp + 2, n_tp)
+        mate, cross = {"tp": mate_tp}, {"tp": cross_tp}
+        mine = tp // 2
         weights = (wk, wv, wq, wg)
 
         barrier = pltpu.get_barrier_semaphore()
         pl.semaphore_signal(barrier, inc=1, device_id=partner)
-        for k in range(1, n_tp):
-            pl.semaphore_signal(barrier, inc=1, device_id={"tp": lax.rem(tp + k, n_tp)})
+        pl.semaphore_signal(barrier, inc=1, device_id=mate)
+        pl.semaphore_signal(barrier, inc=1, device_id=cross)
 
         def greet(k, carry):
             pl.semaphore_signal(barrier, inc=1, device_id={"ctx": lax.rem(ctx + k, n_ctx)})
@@ -89,7 +94,7 @@
         abuf[...] = jnp.broadcast_to(total, abuf.shape)
         arcv[ctx] = jnp.broadcast_to(total, abuf.shape)
 
-        pl.semaphore_wait(barrier, 1 + (n_tp - 1) + n_peers)
+        pl.semaphore_wait(barrier, 3 + n_peers)
 
         def swap(i, h):
             return pltpu.make_async_remote_copy(
@@ -115,42 +120,40 @@
 
         lax.fori_loop(1, n_ctx, send_total, 0)
 
-        per_core = n_tp // 2
-        width = wo.shape[1] // per_core
-
-        def wo_send(j):
-            return pltpu.make_async_remote_copy(
-                src_ref=wo.at[:, j * width : (j + 1) * width],
-                dst_ref=wov.at[tp],
-                send_sem=wosend.at[j],
-                recv_sem=worecv.at[tp],
-                device_id={"tp": per_core * core + j},
-            )
-
-        def wo_own(j):
-            return pltpu.make_async_copy(
-                wo.at[:, j * width : (j + 1) * width], wov.at[tp], wolocal
-            )
-
-        def wo_from(r):
-            return pltpu.make_async_remote_copy(
-                src_ref=wov.at[r],
-                dst_ref=wov.at[r],
-                send_sem=wofwd.at[r],
-                recv_sem=worecv.at[r],
-                device_id=partner,
-            )
-
-        for j in range(per_core):
-            here = per_core * core + j == tp
-
-            @pl.when(jnp.logical_not(here))
-            def _():
-                wo_send(j).start()
-
-            @pl.when(here)
-            def _():
-                wo_own(j).start()
+        width = wo.shape[1] // 2
+        group = lax.rem((tp + 1) // 2, 2)
+        near = group + core * (1 - 2 * group)
+
+        def wo_columns(index):
+            return wo.at[:, pl.ds(pl.multiple_of(index * width, width), width)]
+
+        def wo_own():
+            return pltpu.make_async_copy(wo_columns(near), wov.at[core, tp], wolocal)
+
+        def wo_copy(source, r, k, to):
+            return pltpu.make_async_remote_copy(
+                src_ref=source, dst_ref=wov.at[core, r], send_sem=wosend.at[k],
+                recv_sem=worecv.at[k], device_id=to,
+            )
+
+        def wo_cross():
+            return wo_copy(wo_columns(near), tp, 0, cross)
+
+        def wo_mate():
+            return wo_copy(wo_columns(1 - near), tp, 1, mate)
+
+        def wo_relay():
+            return wo_copy(wov.at[core, mate_tp], mate_tp, 2, cross)
+
+        def wo_hand(r):
+            return pltpu.make_async_remote_copy(
+                src_ref=wov.at[core, r], dst_ref=wov.at[core, r], send_sem=wofwd.at[r],
+                recv_sem=wogot.at[r], device_id=partner,
+            )
+
+        wo_own().start()
+        wo_mate().start()
+        wo_cross().start()
 
         cc, sc = cos_c[pl.ds(ctx, 1), :], sin_c[pl.ds(ctx, 1), :]
         cosv[0:32, :] = cos_a[...] * cc - sin_a[...] * sc
@@ -274,48 +277,53 @@
                     mixed = jnp.where(t >= s, scores * decay, 0.0).astype(BF16)
                     ret[h, mine] = dot(mixed, vb[h, seen])
 
-        def ag_own(h, b, way):
-            return pltpu.make_async_remote_copy(
-                src_ref=hid.at[tp, h, b],
-                dst_ref=hid.at[tp, h, b],
-                send_sem=agsend.at[way, h, b],
-                recv_sem=agrecv.at[way, h, b],
-                device_id=right if way == 0 else left,
-            )
-
-        def ag_forward(h, way):
-            source = lax.rem(tp + (n_tp - 1 if way == 0 else 1), n_tp)
-            return pltpu.make_async_remote_copy(
-                src_ref=hid.at[source, h, way],
-                dst_ref=hid.at[source, h, way],
-                send_sem=fwsend.at[way, h],
-                recv_sem=fwrecv.at[way, h],
-                device_id=right if way == 0 else left,
-            )
+        def piece(p):
+            return pl.ds(p * PIECE, PIECE)
+
+        def hidden_copy(source, owner, h, p, sends, receives, to):
+            return pltpu.make_async_remote_copy(
+                src_ref=source, dst_ref=hid.at[owner, h, piece(p)], send_sem=sends.at[h, p],
+                recv_sem=receives.at[h, p], device_id=to,
+            )
+
+        def to_cross(h, p):
+            return hidden_copy(away.at[h, piece(p)], tp, h, p, crsend, crrecv, cross)
+
+        def to_mate(h, p):
+            return hidden_copy(hid.at[tp, h, piece(p)], tp, h, p, mtsend, mtrecv, mate)
+
+        def forward(h, p):
+            source = hid.at[cross_tp, h, piece(p)]
+            return hidden_copy(source, cross_tp, h, p, fwsend, fwrecv, mate)
 
         def finish(h):
             many(sbuf.at[h], psend.at[h], precv.at[h]).wait_recv()
             state = jnp.concatenate(
                 [sbuf[h, j * 16 : (j + 1) * 16].reshape(DH, HALF) for j in range(2)], axis=1
             )
-            later = (jnp.exp(block_end(h, 0)) * state.astype(F32) + ust[h, 0]).astype(BF16)
-            for b in range(2):
-                prior = state if b == 0 else later
-                inter = jnp.exp(decay_column(h, b)) * dot(qb[h, positions(b)], prior)
-                retained = ret[h, positions(b)] + inter
+            stv[0] = state
+            stv[1] = (jnp.exp(block_end(h, 0)) * state.astype(F32) + ust[h, 0]).astype(BF16)
+
+            def hidden(b):
+                at = pl.ds(pl.multiple_of(b * BLOCK, BLOCK), BLOCK)
+                inter = jnp.exp(ccol[at, h : h + 1]) * dot(qb[h, at], stv[b])
+                retained = ret[h, at] + inter
                 center = retained - jnp.mean(retained, axis=-1, keepdims=True)
                 spread = jnp.mean(center * center, axis=-1, keepdims=True)
                 normed = center * lax.rsqrt(spread + 1e-5)
-                gates = gb[h, positions(b)].astype(F32)
+                gates = gb[h, at].astype(F32)
                 silu = gates / (1.0 + jnp.exp(-gates))
-                hid[tp, h, b] = (silu * normed).astype(BF16)
-                ag_own(h, b, b).start()
-            ag_own(h, 1, 0).start()
-            ag_own(h, 0, 1).start()
-
-        def fold(source, h, b, first=False):
-            product = dot(hid[source, h, b], wov[source, h * DH : (h + 1) * DH, :])
-            oacc[b] = product if first else oacc[b] + product
+                return (silu * normed).astype(BF16)
+
+            away[h] = hidden(1 - mine)
+            for p in range(PIECES):
+                to_cross(h, p).start()
+            hid[tp, h] = hidden(mine)
+
+        def fold(source, h, at=slice(None), first=False):
+            for slot in range(2):
+                product = dot(hid[source, h, at], wov[slot, source, h * DH : (h + 1) * DH, :])
+                oacc[slot, at] = product if first else oacc[slot, at] + product
 
         tok_copy(0).wait()
         own_product(KEY, 0)
@@ -326,94 +334,88 @@
         query_gate(0)
         intra(0)
         many(arcv, asend, arecv).wait_recv()
+        wo_mate().wait_recv()
+        wo_relay().start()
         scan(0)
         key_value(1)
         states(1)
         query_gate(1)
         finish(0)
-
-        holder = tp // per_core == core
-        for j in range(per_core):
-            @pl.when(per_core * core + j == tp)
-            def _():
-                wo_own(j).wait()
-
-        @pl.when(holder)
-        def _():
-            wo_from(tp).start()
-
-        for k in range(1, n_tp):
-            r = lax.rem(tp + k, n_tp)
-
-            @pl.when(holder)
-            def _():
-                wo_from(r).wait_recv()
-                wo_from(r).start()
-
+        for p in range(PIECES):
+            to_mate(0, p).start()
+
+        wo_own().wait()
+        wo_cross().wait_recv()
+        for r in (tp, mate_tp, cross_tp):
+            wo_hand(r).start()
         intra(1)
         scan(1)
-
-        @pl.when(jnp.logical_not(holder))
-        def _():
-            for r in range(n_tp):
-                wo_from(r).wait_recv()
-
-        before, after = lax.rem(tp + n_tp - 1, n_tp), lax.rem(tp + 1, n_tp)
-        opposite = lax.rem(tp + 2, n_tp)
-
-        def neighbours(h):
-            for way in range(2):
-                ag_own(h, way, way).wait_recv()
-                ag_forward(h, way).start()
-            fold(before, h, 0)
-            fold(after, h, 1)
-
-        for b in range(2):
-            fold(tp, 0, b, first=True)
-        neighbours(0)
+        wo_relay().wait_recv()
+        wo_hand(opposite_tp).start()
+        for p in range(PIECES):
+            to_cross(0, p).wait_recv()
+            forward(0, p).start()
+        for r in range(n_tp):
+            wo_hand(r).wait_recv()
+        fold(tp, 0, first=True)
         finish(1)
-        for b in range(2):
-            fold(tp, 1, b)
-        for h in range(2):
-            if h == 1:
-                neighbours(h)
-            ag_own(h, 1, 0).wait_recv()
-            fold(before, h, 1)
-            ag_own(h, 0, 1).wait_recv()
-            fold(after, h, 0)
-            for way in range(2):
-                ag_forward(h, way).wait_recv()
-                fold(opposite, h, way)
-                if h == 1:
-                    obuf[positions(way)] = oacc[way].astype(BF16)
-                    pltpu.make_async_copy(
-                        obuf.at[positions(way)], out.at[positions(way)], osem.at[way]
-                    ).start()
-
-        @pl.when(holder)
-        def _():
-            for r in range(n_tp):
-                wo_from(r).wait_send()
-
-        for j in range(per_core):
-            @pl.when(per_core * core + j != tp)
-            def _():
-                wo_send(j).wait_send()
-
+        for p in range(PIECES):
+            to_mate(1, p).start()
+            to_cross(1, p).wait_recv()
+            forward(1, p).start()
+        fold(tp, 1)
+        fold(cross_tp, 0)
+        fold(cross_tp, 1)
+        for p in range(PIECES):
+            to_mate(0, p).wait_recv()
+        fold(mate_tp, 0)
+        for p in range(PIECES):
+            forward(0, p).wait_recv()
+        fold(opposite_tp, 0)
+
+        def place(p):
+            return out.at[pl.ds(pl.multiple_of(mine * BLOCK + p * PIECE, PIECE), PIECE)]
+
+        def keep(p):
+            return pltpu.make_async_copy(obuf.at[mine, piece(p)], place(p), osem.at[p])
+
+        def give(p):
+            return pltpu.make_async_remote_copy(
+                src_ref=obuf.at[1 - mine, piece(p)], dst_ref=place(p), send_sem=p2send.at[p],
+                recv_sem=p2recv.at[p], device_id=cross,
+            )
+
+        for p in range(PIECES):
+            to_mate(1, p).wait_recv()
+            forward(1, p).wait_recv()
+            at = slice(p * PIECE, (p + 1) * PIECE)
+            for slot in range(2):
+                last = oacc[slot, at]
+                for source in (mate_tp, opposite_tp):
+                    last += dot(hid[source, 1, at], wov[slot, source, DH : 2 * DH, :])
+                obuf[slot, at] = last.astype(BF16)
+            give(p).start()
+            keep(p).start()
+
+        wo_cross().wait_send()
+        wo_mate().wait_send()
+        wo_relay().wait_send()
+        for r in range(n_tp):
+            wo_hand(r).wait_send()
         for i, h in order:
             swap(i, h).wait_send()
         many(arcv, asend, arecv).wait_send()
         for h in range(2):
             many(rbuf.at[h], usend.at[h], urecv.at[h]).wait_send()
             many(sbuf.at[h], psend.at[h], precv.at[h]).wait_send()
-            for way in range(2):
-                for b in range(2):
-                    ag_own(h, b, way).wait_send()
-                ag_forward(h, way).wait_send()
-        for way in range(2):
-            pltpu.make_async_copy(
-                obuf.at[positions(way)], out.at[positions(way)], osem.at[way]
-            ).wait()
+            for p in range(PIECES):
+                to_cross(h, p).wait_send()
+                to_mate(h, p).wait_send()
+                forward(h, p).wait_send()
+        for p in range(PIECES):
+            keep(p).wait()
+            give(p).wait_send()
+            give(p).wait_recv()
 
     return kernel
 
@@ -438,7 +440,7 @@
             scratch_shapes=[
                 vmem(rows, depth),
                 vmem(4, 2, depth, DH),
-                vmem(n_tp, out_rows, cols),
+                vmem(2, n_tp, out_rows, cols),
                 vmem(2, rows, DH, dtype=F32),
                 vmem(2, rows, DH),
                 vmem(2, rows, DH),
@@ -456,13 +458,16 @@
                 vmem(rows, 8, dtype=F32),
                 vmem(rows, HALF, dtype=F32),
                 vmem(rows, HALF, dtype=F32),
-                vmem(n_tp, 2, 2, BLOCK, DH),
+                vmem(2, DH, DH),
+                vmem(n_tp, 2, BLOCK, DH),
+                vmem(2, BLOCK, DH),
                 vmem(2, BLOCK, cols, dtype=F32),
-                vmem(rows, cols),
+                vmem(2, BLOCK, cols),
                 dma(2), dma(4, 2), dma(4, 2), dma(4, 2), dma(), dma(),
                 dma(2), dma(2), dma(2), dma(2),
-                dma(), dma(2), dma(n_tp), dma(n_tp),
-                dma(2, 2, 2), dma(2, 2, 2), dma(2, 2), dma(2, 2), dma(2),
+                dma(), dma(3), dma(3), dma(n_tp), dma(n_tp),
+                dma(2, PIECES), dma(2, PIECES), dma(2, PIECES), dma(2, PIECES),
+                dma(2, PIECES), dma(2, PIECES), dma(PIECES), dma(PIECES), dma(PIECES),
             ],
             compiler_params=pltpu.CompilerParams(
                 collective_id=0, has_side_effects=True, vmem_limit_bytes=60 << 20

time: 73.9 us -> 68.1 us (0.922); the launches traced: 72.8 us -> 67.9 us
  Pallas kernels: 70.5 us -> 65.6 us
    pallas_call x1, Pallas kernels: 70.5 us -> 65.6 us  [on_device(): pl.pallas_call(make_kernel(n_ctx, n_tp), out_shape=jax.ShapeDtypeStruct((...]
where the time goes in v3:
time: 68.1 us; the launch traced here: 67.9 us
  Pallas kernels  65.6 us (96%)
  local copies, waits for them, and re-layouts  2.26 us (3%)
    pallas_call x1, Pallas kernels, on_device(): pl.pallas_call(make_kernel(n_ctx, n_tp), out_shape=jax.ShapeDtypeStruct((...  65.6 us
    unnamed x1, local copies, waits for them, and re-layouts  2.26 us

profile of v3, /device:TPU:8, one launch (start us, length us, event | category | flops | bytes accessed | tf_op | source)
XLA Modules:
  0.0 67.9 jit_solution(11505543238873149600)
XLA Ops:
  0.0 65.6 %retention.1 = bf16[1024,512]{1,0:T(8,128)(2,1)} custom-call(bf16[1024,2048]{1,0:T(8,128)(2,1)} %bitcast.6, bf16[1024,512]{1,0:T(8,128)(2,1)} %wk.1, bf16[1024,512]{1,0:T(8,128)(2,1)} %wv.1, bf16[1024,512]{1,0:T(8,128)(2,1)} %wq.1, bf16[1024,512]{1,0:T(8,128)(2,1)} %wg.1, bf16[512,1024]{1,0:T(8,128)(2,1)} %wo.1, f32[2,1024]{1,0:T(2,128)} %bitcast.7, ...), custom_call_target="tpu_custom_call" | custom-call | tf_op jit(solution)/shard_map/retention/pallas_call | solution.py:435
  65.6 2.3 %copy.15 = bf16[1,1024,512]{2,1,0:T(8,128)(2,1)} copy(bf16[1,1024,512]{2,1,0:T(8,128)(2,1)} %bitcast.5) | data formatting | bytes 2097152

commit v4 on v3

--- a/solution.py
+++ b/solution.py
@@ -25,19 +25,22 @@
     for stride, count in ((32, rows // 32), (1, 32), (rows, ctx_count)):
         angles = (np.arange(count) * stride)[:, None] * frequency[None, :]
         tables += [np.cos(angles), np.sin(angles)]
-    return [t.astype(np.float32) for t in tables]
+    return np.concatenate(tables).astype(np.float32)
 
 
 def make_kernel(n_ctx, n_tp):
     n_peers = n_ctx - 1
 
+    def offset(i):
+        return n_ctx // 2 + (i // 2 + lax.rem(i, 2)) * (1 - 2 * lax.rem(i, 2))
+
     def kernel(
-        tok, wk, wv, wq, wg, wo, ld, cos_a, sin_a, cos_b, sin_b, cos_c, sin_c, out,
-        tokv, wv_all, wov, acc, kb, vb, qb, gb, ret, ust, ubuf, rbuf, pbuf, sbuf,
+        tok, wk, wv, wq, wg, wo, ld, turns, out,
+        logs, table, tokv, wv_all, wov, acc, kb, vb, qb, gb, ret, ust, ubuf, rbuf, pbuf, sbuf,
         abuf, arcv, crow, ccol, cosv, sinv, stv, hid, away, oacc, obuf,
-        tsem, lsem, wsend, wrecv, asend, arecv, usend, urecv, psend, precv,
+        isem, tsem, lsem, wsend, wrecv, asend, arecv, usend, urecv, psend, precv,
         wolocal, wosend, worecv, wofwd, wogot, crsend, crrecv, mtsend, mtrecv,
-        fwsend, fwrecv, p2send, p2recv, osem,
+        fwsend, fwrecv, p2send, p2recv,
     ):
         ctx, tp, core = (lax.axis_index(n) for n in ("ctx", "tp", "fsdp"))
         rows = tok.shape[0]
@@ -50,15 +53,23 @@
         weights = (wk, wv, wq, wg)
 
         barrier = pltpu.get_barrier_semaphore()
+        def greet(k, carry):
+            pl.semaphore_signal(barrier, inc=1, device_id={"ctx": lax.rem(ctx + offset(k), n_ctx)})
+            return carry
+
+        lax.fori_loop(0, n_peers, greet, 0)
         pl.semaphore_signal(barrier, inc=1, device_id=partner)
         pl.semaphore_signal(barrier, inc=1, device_id=mate)
         pl.semaphore_signal(barrier, inc=1, device_id=cross)
 
-        def greet(k, carry):
-            pl.semaphore_signal(barrier, inc=1, device_id={"ctx": lax.rem(ctx + k, n_ctx)})
-            return carry
-
-        lax.fori_loop(1, n_ctx, greet, 0)
+        def log_copy():
+            return pltpu.make_async_copy(ld, logs, isem.at[0])
+
+        def table_copy():
+            return pltpu.make_async_copy(turns, table, isem.at[1])
+
+        log_copy().start()
+        table_copy().start()
 
         own_rows = pl.ds(pl.multiple_of(core * khalf, khalf), khalf)
         other_rows = pl.ds(pl.multiple_of((1 - core) * khalf, khalf), khalf)
@@ -71,7 +82,7 @@
             source = weights[i].at[:, h * DH : (h + 1) * DH]
             return pltpu.make_async_copy(source, wv_all.at[i, h, own_rows], lsem.at[i, h])
 
-        order = [(KEY, 0), (VALUE, 0), (QUERY, 0), (GATE, 0), (KEY, 1), (VALUE, 1), (QUERY, 1), (GATE, 1)]
+        order = [(KEY, 0), (VALUE, 0), (KEY, 1), (VALUE, 1), (QUERY, 0), (GATE, 0), (QUERY, 1), (GATE, 1)]
         tok_copy(0).start()
         for i, h in order[:2]:
             own_copy(i, h).start()
@@ -80,7 +91,8 @@
             own_copy(i, h).start()
 
         crow[...] = jnp.zeros_like(crow)
-        crow[0 : ld.shape[0], :] = ld[...]
+        log_copy().wait()
+        crow[0 : logs.shape[0], :] = logs[...]
         running = crow[...]
         lane = lax.rem(lax.broadcasted_iota(jnp.int32, running.shape, 1), BLOCK)
         step = 1
@@ -114,11 +126,11 @@
                 dst_ref=arcv.at[ctx],
                 send_sem=asend,
                 recv_sem=arecv,
-                device_id={"ctx": lax.rem(ctx + k, n_ctx)},
+                device_id={"ctx": lax.rem(ctx + offset(k), n_ctx)},
             ).start()
             return carry
 
-        lax.fori_loop(1, n_ctx, send_total, 0)
+        lax.fori_loop(0, n_peers, send_total, 0)
 
         width = wo.shape[1] // 2
         group = lax.rem((tp + 1) // 2, 2)
@@ -155,14 +167,17 @@
         wo_mate().start()
         wo_cross().start()
 
-        cc, sc = cos_c[pl.ds(ctx, 1), :], sin_c[pl.ds(ctx, 1), :]
-        cosv[0:32, :] = cos_a[...] * cc - sin_a[...] * sc
-        sinv[0:32, :] = sin_a[...] * cc + cos_a[...] * sc
-        base_cos, base_sin = cosv[0:32, :], sinv[0:32, :]
+        table_copy().wait()
+        fine = rows // 32
+        cos_a, sin_a = table[0:fine, :], table[fine : 2 * fine, :]
+        cos_b, sin_b = (table[2 * fine + k * 32 : 2 * fine + (k + 1) * 32, :] for k in range(2))
+        base = 2 * fine + 64
+        cc, sc = (table[pl.ds(base + k * n_ctx + ctx, 1), :] for k in range(2))
+        base_cos, base_sin = cos_a * cc - sin_a * sc, sin_a * cc + cos_a * sc
         for a in range(rows // 32):
             ca, sa = base_cos[a : a + 1, :], base_sin[a : a + 1, :]
-            cosv[a * 32 : (a + 1) * 32, :] = ca * cos_b[...] - sa * sin_b[...]
-            sinv[a * 32 : (a + 1) * 32, :] = sa * cos_b[...] + ca * sin_b[...]
+            cosv[a * 32 : (a + 1) * 32, :] = ca * cos_b - sa * sin_b
+            sinv[a * 32 : (a + 1) * 32, :] = sa * cos_b + ca * sin_b
 
         def positions(b):
             return slice(b * BLOCK, (b + 1) * BLOCK)
@@ -191,8 +206,10 @@
             kb[h, :, :HALF], kb[h, :, HALF:] = rotated(project(KEY, h, split))
             vb[h] = project(VALUE, h, split).astype(BF16)
 
-        def query_gate(h):
+        def query(h):
             qb[h, :, :HALF], qb[h, :, HALF:] = rotated(project(QUERY, h))
+
+        def gate(h):
             gb[h] = project(GATE, h).astype(BF16)
 
         def block_end(h, b):
@@ -215,7 +232,7 @@
             rbuf[h, ctx] = ubuf[h, ctx]
 
             def send(k, carry):
-                to = lax.rem(ctx + k, n_ctx)
+                to = lax.rem(ctx + offset(k), n_ctx)
                 pltpu.make_async_remote_copy(
                     src_ref=ubuf.at[h, to],
                     dst_ref=rbuf.at[h, ctx],
@@ -225,7 +242,7 @@
                 ).start()
                 return carry
 
-            lax.fori_loop(1, n_ctx, send, 0)
+            lax.fori_loop(0, n_peers, send, 0)
 
         def many(buffer, send_sem, recv_sem):
             part = buffer.at[pl.ds(0, n_peers)]
@@ -237,15 +254,14 @@
         def scan(h):
             many(rbuf.at[h], usend.at[h], urecv.at[h]).wait_recv()
 
-            def hop(d, before):
+            before = jnp.zeros((16, HALF), F32)
+            for d in range(n_ctx):
                 pbuf[h, d] = before.astype(BF16)
-                return before * jnp.exp(arcv[d, h : h + 1, :]) + rbuf[h, d].astype(F32)
-
-            lax.fori_loop(0, n_ctx, hop, jnp.zeros((16, HALF), F32))
+                before = before * jnp.exp(arcv[d, h : h + 1, :]) + rbuf[h, d].astype(F32)
             sbuf[h, ctx] = pbuf[h, ctx]
 
             def send(k, carry):
-                to = lax.rem(ctx + k, n_ctx)
+                to = lax.rem(ctx + offset(k), n_ctx)
                 pltpu.make_async_remote_copy(
                     src_ref=pbuf.at[h, to],
                     dst_ref=sbuf.at[h, ctx],
@@ -255,7 +271,7 @@
                 ).start()
                 return carry
 
-            lax.fori_loop(1, n_ctx, send, 0)
+            lax.fori_loop(0, n_peers, send, 0)
 
         quarter = BLOCK // 2
 
@@ -331,15 +347,18 @@
         tok_copy(1).wait()
         key_value(0)
         states(0)
-        query_gate(0)
-        intra(0)
-        many(arcv, asend, arecv).wait_recv()
+        key_value(1)
+        states(1)
+        query(0)
         wo_mate().wait_recv()
         wo_relay().start()
+        many(arcv, asend, arecv).wait_recv()
         scan(0)
-        key_value(1)
-        states(1)
-        query_gate(1)
+        gate(0)
+        intra(0)
+        scan(1)
+        query(1)
+        gate(1)
         finish(0)
         for p in range(PIECES):
             to_mate(0, p).start()
@@ -349,39 +368,40 @@
         for r in (tp, mate_tp, cross_tp):
             wo_hand(r).start()
         intra(1)
-        scan(1)
-        wo_relay().wait_recv()
-        wo_hand(opposite_tp).start()
+        finish(1)
         for p in range(PIECES):
             to_cross(0, p).wait_recv()
             forward(0, p).start()
-        for r in range(n_tp):
+            if p == 0:
+                wo_relay().wait_recv()
+                wo_hand(opposite_tp).start()
+                wo_hand(tp).wait_recv()
+            if p == 1:
+                fold(tp, 0, first=True)
+                fold(tp, 1)
+        for r in (cross_tp, mate_tp, opposite_tp):
             wo_hand(r).wait_recv()
-        fold(tp, 0, first=True)
-        finish(1)
         for p in range(PIECES):
             to_mate(1, p).start()
             to_cross(1, p).wait_recv()
             forward(1, p).start()
-        fold(tp, 1)
-        fold(cross_tp, 0)
+            if p == 0:
+                fold(cross_tp, 0)
+            if p == 1:
+                for q in range(PIECES):
+                    to_mate(0, q).wait_recv()
+                fold(mate_tp, 0)
         fold(cross_tp, 1)
-        for p in range(PIECES):
-            to_mate(0, p).wait_recv()
-        fold(mate_tp, 0)
         for p in range(PIECES):
             forward(0, p).wait_recv()
         fold(opposite_tp, 0)
 
         def place(p):
-            return out.at[pl.ds(pl.multiple_of(mine * BLOCK + p * PIECE, PIECE), PIECE)]
-
-        def keep(p):
-            return pltpu.make_async_copy(obuf.at[mine, piece(p)], place(p), osem.at[p])
+            return pl.ds(pl.multiple_of(mine * BLOCK + p * PIECE, PIECE), PIECE)
 
         def give(p):
             return pltpu.make_async_remote_copy(
-                src_ref=obuf.at[1 - mine, piece(p)], dst_ref=place(p), send_sem=p2send.at[p],
+                src_ref=obuf.at[piece(p)], dst_ref=out.at[place(p)], send_sem=p2send.at[p],
                 recv_sem=p2recv.at[p], device_id=cross,
             )
 
@@ -389,13 +409,16 @@
             to_mate(1, p).wait_recv()
             forward(1, p).wait_recv()
             at = slice(p * PIECE, (p + 1) * PIECE)
-            for slot in range(2):
+
+            def total_of(slot):
                 last = oacc[slot, at]
                 for source in (mate_tp, opposite_tp):
                     last += dot(hid[source, 1, at], wov[slot, source, DH : 2 * DH, :])
-                obuf[slot, at] = last.astype(BF16)
+                return last.astype(BF16)
+
+            obuf[at] = total_of(1 - mine)
             give(p).start()
-            keep(p).start()
+            out[place(p)] = total_of(mine)
 
         wo_cross().wait_send()
         wo_mate().wait_send()
@@ -413,7 +436,6 @@
                 to_mate(h, p).wait_send()
                 forward(h, p).wait_send()
         for p in range(PIECES):
-            keep(p).wait()
             give(p).wait_send()
             give(p).wait_recv()
 
@@ -434,10 +456,12 @@
         small = pl.BlockSpec(memory_space=pltpu.VMEM)
         result = pl.pallas_call(
             make_kernel(n_ctx, n_tp),
-            out_shape=jax.ShapeDtypeStruct((rows, cols), BF16),
-            in_specs=[anywhere] * 6 + [small] * 7,
-            out_specs=anywhere,
+            out_shape=pltpu.VMEM((rows, cols), BF16),
+            in_specs=[anywhere] * 8,
+            out_specs=small,
             scratch_shapes=[
+                vmem(cols // DH, rows, dtype=F32),
+                vmem(*tables.shape, dtype=F32),
                 vmem(rows, depth),
                 vmem(4, 2, depth, DH),
                 vmem(2, n_tp, out_rows, cols),
@@ -462,12 +486,12 @@
                 vmem(n_tp, 2, BLOCK, DH),
                 vmem(2, BLOCK, DH),
                 vmem(2, BLOCK, cols, dtype=F32),
-                vmem(2, BLOCK, cols),
-                dma(2), dma(4, 2), dma(4, 2), dma(4, 2), dma(), dma(),
+                vmem(BLOCK, cols),
+                dma(2), dma(2), dma(4, 2), dma(4, 2), dma(4, 2), dma(), dma(),
                 dma(2), dma(2), dma(2), dma(2),
                 dma(), dma(3), dma(3), dma(n_tp), dma(n_tp),
                 dma(2, PIECES), dma(2, PIECES), dma(2, PIECES), dma(2, PIECES),
-                dma(2, PIECES), dma(2, PIECES), dma(PIECES), dma(PIECES), dma(PIECES),
+                dma(2, PIECES), dma(2, PIECES), dma(PIECES), dma(PIECES),
             ],
             compiler_params=pltpu.CompilerParams(
                 collective_id=0, has_side_effects=True, vmem_limit_bytes=60 << 20
@@ -475,7 +499,7 @@
             name="retention",
         )(
             tokens[0], key_weight, value_weight, query_weight, gate_weight, out_weight,
-            jnp.transpose(log_decay[0]), *tables,
+            jnp.transpose(log_decay[0]), tables,
         )
         return result[None]
 

time: 68.1 us -> 66.1 us (0.971)
  local copies, waits for them, and re-layouts: 2.26 us -> 0.97 us
  Pallas kernels: 65.6 us -> 64.5 us
    unnamed x1, local copies, waits for them, and re-layouts: 2.26 us -> 0.97 us
    pallas_call x1, Pallas kernels: 65.6 us -> 64.5 us  [on_device(): pl.pallas_call(make_kernel(n_ctx, n_tp), out_shape=pltpu.VMEM((rows, cols...]
where the time goes in v4:
time: 66.1 us; the launch traced here: 65.4 us
  Pallas kernels  64.5 us (98%)
  local copies, waits for them, and re-layouts  0.97 us (1%)
    pallas_call x1, Pallas kernels, on_device(): pl.pallas_call(make_kernel(n_ctx, n_tp), out_shape=pltpu.VMEM((rows, cols...  64.5 us

profile of v4, /device:TPU:8, one launch (start us, length us, event | category | flops | bytes accessed | tf_op | source)
XLA Modules:
  0.0 65.4 jit_solution(6721611719263700665)
XLA Ops:
  0.0 64.5 %retention.1 = bf16[1024,512]{1,0:T(8,128)(2,1)S(1)} custom-call(bf16[1024,2048]{1,0:T(8,128)(2,1)} %bitcast.6, bf16[1024,512]{1,0:T(8,128)(2,1)} %wk.1, bf16[1024,512]{1,0:T(8,128)(2,1)} %wv.1, bf16[1024,512]{1,0:T(8,128)(2,1)} %wq.1, bf16[1024,512]{1,0:T(8,128)(2,1)} %wg.1, bf16[512,1024]{1,0:T(8,128)(2,1)} %wo.1, f32[2,1024]{1,0:T(2,128)} %bitcast.7, ...), custom_call_target="tpu_custom_call" | custom-call | tf_op jit(solution)/shard_map/retention/pallas_call | solution.py:457
  64.5 1.0 %copy.10 = bf16[1,1024,512]{2,1,0:T(8,128)(2,1)} copy(bf16[1,1024,512]{2,1,0:T(8,128)(2,1)S(1)} %bitcast.5) | data formatting | bytes 2097152

commit v5 on v4

--- a/solution.py
+++ b/solution.py
@@ -142,20 +142,25 @@
         def wo_own():
             return pltpu.make_async_copy(wo_columns(near), wov.at[core, tp], wolocal)
 
-        def wo_copy(source, r, k, to):
+        def wo_copy(source, target, k, to):
             return pltpu.make_async_remote_copy(
-                src_ref=source, dst_ref=wov.at[core, r], send_sem=wosend.at[k],
+                src_ref=source, dst_ref=target, send_sem=wosend.at[k],
                 recv_sem=worecv.at[k], device_id=to,
             )
 
         def wo_cross():
-            return wo_copy(wo_columns(near), tp, 0, cross)
-
-        def wo_mate():
-            return wo_copy(wo_columns(1 - near), tp, 1, mate)
-
-        def wo_relay():
-            return wo_copy(wov.at[core, mate_tp], mate_tp, 2, cross)
+            return wo_copy(wo_columns(near), wov.at[core, tp], 4, cross)
+
+        part_rows = wo.shape[0] // 2
+
+        def wo_mate(part):
+            at = pl.ds(part * part_rows, part_rows)
+            columns = pl.ds(pl.multiple_of((1 - near) * width, width), width)
+            return wo_copy(wo.at[at, columns], wov.at[core, tp, at], part, mate)
+
+        def wo_relay(part):
+            block = wov.at[core, mate_tp, pl.ds(part * part_rows, part_rows)]
+            return wo_copy(block, block, 2 + part, cross)
 
         def wo_hand(r):
             return pltpu.make_async_remote_copy(
@@ -164,7 +169,8 @@
             )
 
         wo_own().start()
-        wo_mate().start()
+        for part in range(2):
+            wo_mate(part).start()
         wo_cross().start()
 
         table_copy().wait()
@@ -350,15 +356,16 @@
         key_value(1)
         states(1)
         query(0)
-        wo_mate().wait_recv()
-        wo_relay().start()
+        wo_mate(0).wait_recv()
+        wo_relay(0).start()
         many(arcv, asend, arecv).wait_recv()
         scan(0)
         gate(0)
+        wo_mate(1).wait_recv()
+        wo_relay(1).start()
         intra(0)
         scan(1)
         query(1)
-        gate(1)
         finish(0)
         for p in range(PIECES):
             to_mate(0, p).start()
@@ -367,13 +374,15 @@
         wo_cross().wait_recv()
         for r in (tp, mate_tp, cross_tp):
             wo_hand(r).start()
+        gate(1)
         intra(1)
         finish(1)
         for p in range(PIECES):
             to_cross(0, p).wait_recv()
             forward(0, p).start()
             if p == 0:
-                wo_relay().wait_recv()
+                for part in range(2):
+                    wo_relay(part).wait_recv()
                 wo_hand(opposite_tp).start()
                 wo_hand(tp).wait_recv()
             if p == 1:
@@ -421,8 +430,9 @@
             out[place(p)] = total_of(mine)
 
         wo_cross().wait_send()
-        wo_mate().wait_send()
-        wo_relay().wait_send()
+        for part in range(2):
+            wo_mate(part).wait_send()
+            wo_relay(part).wait_send()
         for r in range(n_tp):
             wo_hand(r).wait_send()
         for i, h in order:
@@ -489,7 +499,7 @@
                 vmem(BLOCK, cols),
                 dma(2), dma(2), dma(4, 2), dma(4, 2), dma(4, 2), dma(), dma(),
                 dma(2), dma(2), dma(2), dma(2),
-                dma(), dma(3), dma(3), dma(n_tp), dma(n_tp),
+                dma(), dma(5), dma(5), dma(n_tp), dma(n_tp),
                 dma(2, PIECES), dma(2, PIECES), dma(2, PIECES), dma(2, PIECES),
                 dma(2, PIECES), dma(2, PIECES), dma(PIECES), dma(PIECES),
             ],

time: 66.1 us -> 64.5 us (0.976)
  Pallas kernels: 64.5 us -> 62.9 us
    pallas_call x1, Pallas kernels: 64.5 us -> 62.9 us  [on_device(): pl.pallas_call(make_kernel(n_ctx, n_tp), out_shape=pltpu.VMEM((rows, cols...]
where the time goes in v5:
time: 64.5 us; the launch traced here: 63.9 us
  Pallas kernels  62.9 us (98%)
  local copies, waits for them, and re-layouts  0.97 us (2%)
    pallas_call x1, Pallas kernels, on_device(): pl.pallas_call(make_kernel(n_ctx, n_tp), out_shape=pltpu.VMEM((rows, cols...  62.9 us

profile of v5, /device:TPU:8, one launch (start us, length us, event | category | flops | bytes accessed | tf_op | source)
XLA Modules:
  0.0 63.9 jit_solution(6903102926251052761)
XLA Ops:
  0.0 62.9 %retention.1 = bf16[1024,512]{1,0:T(8,128)(2,1)S(1)} custom-call(bf16[1024,2048]{1,0:T(8,128)(2,1)} %bitcast.6, bf16[1024,512]{1,0:T(8,128)(2,1)} %wk.1, bf16[1024,512]{1,0:T(8,128)(2,1)} %wv.1, bf16[1024,512]{1,0:T(8,128)(2,1)} %wq.1, bf16[1024,512]{1,0:T(8,128)(2,1)} %wg.1, bf16[512,1024]{1,0:T(8,128)(2,1)} %wo.1, f32[2,1024]{1,0:T(2,128)} %bitcast.7, ...), custom_call_target="tpu_custom_call" | custom-call | tf_op jit(solution)/shard_map/retention/pallas_call | solution.py:467
  62.9 1.0 %copy.10 = bf16[1,1024,512]{2,1,0:T(8,128)(2,1)} copy(bf16[1,1024,512]{2,1,0:T(8,128)(2,1)S(1)} %bitcast.5) | data formatting | bytes 2097152

commit v6 on v5

--- a/solution.py
+++ b/solution.py
@@ -9,7 +9,7 @@
 DH = 256
 HALF = DH // 2
 BLOCK = 512
-PIECES = 4
+PIECES = 8
 PIECE = BLOCK // PIECES
 KEY, VALUE, QUERY, GATE = range(4)
 F32, BF16 = jnp.float32, jnp.bfloat16
@@ -337,10 +337,19 @@
                 silu = gates / (1.0 + jnp.exp(-gates))
                 return (silu * normed).astype(BF16)
 
-            away[h] = hidden(1 - mine)
-            for p in range(PIECES):
-                to_cross(h, p).start()
-            hid[tp, h] = hidden(mine)
+            def near_half():
+                hid[tp, h] = hidden(mine)
+                if h == 0:
+                    for p in range(PIECES):
+                        to_mate(h, p).start()
+
+            def far_half():
+                away[h] = hidden(1 - mine)
+                for p in range(PIECES):
+                    to_cross(h, p).start()
+
+            for half in (near_half, far_half) if h == 0 else (far_half, near_half):
+                half()
 
         def fold(source, h, at=slice(None), first=False):
             for slot in range(2):
@@ -367,8 +376,6 @@
         scan(1)
         query(1)
         finish(0)
-        for p in range(PIECES):
-            to_mate(0, p).start()
 
         wo_own().wait()
         wo_cross().wait_recv()
@@ -380,30 +387,26 @@
         for p in range(PIECES):
             to_cross(0, p).wait_recv()
             forward(0, p).start()
+            to_mate(1, p).start()
+            to_cross(1, p).wait_recv()
+            forward(1, p).start()
             if p == 0:
                 for part in range(2):
                     wo_relay(part).wait_recv()
                 wo_hand(opposite_tp).start()
                 wo_hand(tp).wait_recv()
+                fold(tp, 0, first=True)
             if p == 1:
-                fold(tp, 0, first=True)
                 fold(tp, 1)
-        for r in (cross_tp, mate_tp, opposite_tp):
-            wo_hand(r).wait_recv()
-        for p in range(PIECES):
-            to_mate(1, p).start()
-            to_cross(1, p).wait_recv()
-            forward(1, p).start()
-            if p == 0:
-                fold(cross_tp, 0)
-            if p == 1:
+            if p == 3:
+                wo_hand(mate_tp).wait_recv()
                 for q in range(PIECES):
                     to_mate(0, q).wait_recv()
                 fold(mate_tp, 0)
+        wo_hand(cross_tp).wait_recv()
+        fold(cross_tp, 0)
         fold(cross_tp, 1)
-        for p in range(PIECES):
-            forward(0, p).wait_recv()
-        fold(opposite_tp, 0)
+        wo_hand(opposite_tp).wait_recv()
 
         def place(p):
             return pl.ds(pl.multiple_of(mine * BLOCK + p * PIECE, PIECE), PIECE)
@@ -415,14 +418,16 @@
             )
 
         for p in range(PIECES):
+            forward(0, p).wait_recv()
             to_mate(1, p).wait_recv()
             forward(1, p).wait_recv()
             at = slice(p * PIECE, (p + 1) * PIECE)
 
             def total_of(slot):
                 last = oacc[slot, at]
-                for source in (mate_tp, opposite_tp):
-                    last += dot(hid[source, 1, at], wov[slot, source, DH : 2 * DH, :])
+                for source, h in ((opposite_tp, 0), (mate_tp, 1), (opposite_tp, 1)):
+                    rows_of = slice(h * DH, (h + 1) * DH)
+                    last += dot(hid[source, h, at], wov[slot, source, rows_of, :])
                 return last.astype(BF16)
 
             obuf[at] = total_of(1 - mine)

time: 64.5 us -> 65.7 us (1.019)
  Pallas kernels: 62.9 us -> 64 us
    pallas_call x1, Pallas kernels: 62.9 us -> 64 us  [on_device(): pl.pallas_call(make_kernel(n_ctx, n_tp), out_shape=pltpu.VMEM((rows, cols...]
where the time goes in v6:
time: 65.7 us; the launch traced here: 65 us
  Pallas kernels  64 us (97%)
  local copies, waits for them, and re-layouts  0.97 us (1%)
    pallas_call x1, Pallas kernels, on_device(): pl.pallas_call(make_kernel(n_ctx, n_tp), out_shape=pltpu.VMEM((rows, cols...  64 us

profile of v6, /device:TPU:8, one launch (start us, length us, event | category | flops | bytes accessed | tf_op | source)
XLA Modules:
  0.0 65.0 jit_solution(8986289331924789610)
XLA Ops:
  0.0 64.0 %retention.1 = bf16[1024,512]{1,0:T(8,128)(2,1)S(1)} custom-call(bf16[1024,2048]{1,0:T(8,128)(2,1)} %bitcast.6, bf16[1024,512]{1,0:T(8,128)(2,1)} %wk.1, bf16[1024,512]{1,0:T(8,128)(2,1)} %wv.1, bf16[1024,512]{1,0:T(8,128)(2,1)} %wq.1, bf16[1024,512]{1,0:T(8,128)(2,1)} %wg.1, bf16[512,1024]{1,0:T(8,128)(2,1)} %wo.1, f32[2,1024]{1,0:T(2,128)} %bitcast.7, ...), custom_call_target="tpu_custom_call" | custom-call | tf_op jit(solution)/shard_map/retention/pallas_call | solution.py:472
  64.1 1.0 %copy.10 = bf16[1,1024,512]{2,1,0:T(8,128)(2,1)} copy(bf16[1,1024,512]{2,1,0:T(8,128)(2,1)S(1)} %bitcast.5) | data formatting | bytes 2097152

commit v7 on v6

--- a/solution.py
+++ b/solution.py
@@ -9,7 +9,7 @@
 DH = 256
 HALF = DH // 2
 BLOCK = 512
-PIECES = 8
+PIECES = 4
 PIECE = BLOCK // PIECES
 KEY, VALUE, QUERY, GATE = range(4)
 F32, BF16 = jnp.float32, jnp.bfloat16
@@ -384,9 +384,16 @@
         gate(1)
         intra(1)
         finish(1)
-        for p in range(PIECES):
+        ahead = PIECES // 2
+        for p in range(ahead):
             to_cross(0, p).wait_recv()
             forward(0, p).start()
+        wo_hand(tp).wait_recv()
+        fold(tp, 0, first=True)
+        for p in range(PIECES):
+            if p + ahead < PIECES:
+                to_cross(0, p + ahead).wait_recv()
+                forward(0, p + ahead).start()
             to_mate(1, p).start()
             to_cross(1, p).wait_recv()
             forward(1, p).start()
@@ -394,8 +401,6 @@
                 for part in range(2):
                     wo_relay(part).wait_recv()
                 wo_hand(opposite_tp).start()
-                wo_hand(tp).wait_recv()
-                fold(tp, 0, first=True)
             if p == 1:
                 fold(tp, 1)
             if p == 3:

time: 65.7 us -> 64.6 us (0.983)
  Pallas kernels: 64 us -> 62.9 us
    pallas_call x1, Pallas kernels: 64 us -> 62.9 us  [on_device(): pl.pallas_call(make_kernel(n_ctx, n_tp), out_shape=pltpu.VMEM((rows, cols...]
where the time goes in v7:
time: 64.6 us; the launch traced here: 63.9 us
  Pallas kernels  62.9 us (97%)
  local copies, waits for them, and re-layouts  0.97 us (2%)
    pallas_call x1, Pallas kernels, on_device(): pl.pallas_call(make_kernel(n_ctx, n_tp), out_shape=pltpu.VMEM((rows, cols...  62.9 us

profile of v7, /device:TPU:8, one launch (start us, length us, event | category | flops | bytes accessed | tf_op | source)
XLA Modules:
  0.0 63.9 jit_solution(219185142505720373)
XLA Ops:
  0.0 62.9 %retention.1 = bf16[1024,512]{1,0:T(8,128)(2,1)S(1)} custom-call(bf16[1024,2048]{1,0:T(8,128)(2,1)} %bitcast.6, bf16[1024,512]{1,0:T(8,128)(2,1)} %wk.1, bf16[1024,512]{1,0:T(8,128)(2,1)} %wv.1, bf16[1024,512]{1,0:T(8,128)(2,1)} %wq.1, bf16[1024,512]{1,0:T(8,128)(2,1)} %wg.1, bf16[512,1024]{1,0:T(8,128)(2,1)} %wo.1, f32[2,1024]{1,0:T(2,128)} %bitcast.7, ...), custom_call_target="tpu_custom_call" | custom-call | tf_op jit(solution)/shard_map/retention/pallas_call | solution.py:477
  62.9 1.0 %copy.10 = bf16[1,1024,512]{2,1,0:T(8,128)(2,1)} copy(bf16[1,1024,512]{2,1,0:T(8,128)(2,1)S(1)} %bitcast.5) | data formatting | bytes 2097152
